TPU v7x, 256 devices: a whole 4x4x8 slice. The times are simulated.
256 devices in a mesh: freq: 32 (over x, z_lo, core), mz: 8 (over y, z_hi).
Axes of the slice: x: 4, y: 4, z: 8 (z_hi: 2, z_lo: 4; z = z_hi * 4 + z_lo), core: 2. Of those that a mesh axis runs over, the one named last changes fastest.
Arguments:
- intensity: bfloat16 [8, 6144, 4096], P(None, 'freq', 'mz'), may hold values from -6 to 6
- elution: float32 [6144, 64], P(('freq', 'mz')), may hold values from -6 to 6
- loadings: float32 [8, 64], replicated, may hold values from 0.0005 to 0.01
- shifts: int32 [8, 64], replicated, may hold values from 0 to 255
- bin_weight: float32 [6144], replicated, may hold values from 0.25 to 4
Outputs:
- spectral: float32 [64, 4096], P(None, ('mz', 'freq'))
All inputs are finite; a program needn't handle non-finite values.
Results may differ from a plain program's by a relative error of at most 0.0003.
Values may be sent and summed in bfloat16 or wider, within the bound.
A program may use at most 64 MiB of HBM per device.

v0:
```python
import math

import jax
import jax.numpy as jnp
from jax import lax
from jax.sharding import PartitionSpec as P

PRECISE = lax.Precision.HIGHEST


def turn_angle(product, length):
    return 2.0 * math.pi / length * (product % length).astype(jnp.float32)


def cholesky_solve(gram_matrix, numerator):
    factor = jnp.linalg.cholesky(gram_matrix)
    middle = lax.linalg.triangular_solve(factor, numerator, left_side=True, lower=True)
    return lax.linalg.triangular_solve(factor, middle, left_side=True, lower=True, transpose_a=True)


def on_device(intensity, elution, loadings, shifts, bin_weight):
    freq_count = lax.axis_size("freq")
    mz_count = lax.axis_size("mz")
    freq_rank = lax.axis_index("freq")
    mz_rank = lax.axis_index("mz")
    run_count, bin_count, local_mz = intensity.shape
    length = bin_count * freq_count
    components = loadings.shape[1]
    block_len = bin_count // freq_count
    norm_scale = 1.0 / math.sqrt(length)
    dev_ids = jnp.arange(freq_count, dtype=jnp.int32)
    bin_ids = jnp.arange(bin_count, dtype=jnp.int32)
    dev_angle = turn_angle(dev_ids[:, None] * dev_ids[None, :], freq_count)
    cos_dev = jnp.cos(dev_angle)
    sin_dev = jnp.sin(dev_angle)
    my_times = freq_rank * block_len + jnp.arange(block_len, dtype=jnp.int32)
    twiddle = turn_angle(dev_ids[:, None] * my_times[None, :], length)
    twid_cos = jnp.cos(twiddle)[None, :, :, None]
    twid_sin = jnp.sin(twiddle)[None, :, :, None]
    bin_angle = turn_angle(bin_ids[:, None] * bin_ids[None, :], bin_count)
    cos_bin = jnp.cos(bin_angle)
    sin_bin = jnp.sin(bin_angle)
    full_elution = lax.all_gather(elution, ("freq", "mz"), axis=0, tiled=True)
    stacked = full_elution.reshape(freq_count, bin_count, components)
    weights_grid = bin_weight.reshape(bin_count, freq_count)
    weights_mine = lax.dynamic_slice_in_dim(weights_grid, freq_rank, 1, 1)[:, 0]
    bins_mine = freq_rank + freq_count * bin_ids
    row_angle = turn_angle(freq_rank * dev_ids, freq_count)
    part_re = jnp.einsum("p,pqr->qr", jnp.cos(row_angle), stacked, precision=PRECISE)
    part_im = -jnp.einsum("p,pqr->qr", jnp.sin(row_angle), stacked, precision=PRECISE)
    own_twid = turn_angle(freq_rank * bin_ids, length)[:, None]
    turn_re = part_re * jnp.cos(own_twid) + part_im * jnp.sin(own_twid)
    turn_im = part_im * jnp.cos(own_twid) - part_re * jnp.sin(own_twid)
    own_re = (
        jnp.dot(cos_bin, turn_re, precision=PRECISE) + jnp.dot(sin_bin, turn_im, precision=PRECISE)
    ) * norm_scale
    own_im = (
        jnp.dot(cos_bin, turn_im, precision=PRECISE) - jnp.dot(sin_bin, turn_re, precision=PRECISE)
    ) * norm_scale
    weights_col = weights_mine[None, :, None]

    def own_model(run_amp, run_lag):
        phase = turn_angle(bins_mine[None, :, None] * run_lag[:, None, :], length)
        phase_cos = jnp.cos(phase)
        phase_sin = jnp.sin(phase)
        model_re = run_amp[:, None, :] * (own_re * phase_cos + own_im * phase_sin)
        model_im = run_amp[:, None, :] * (own_im * phase_cos - own_re * phase_sin)
        return (model_re, model_im)

    samples = lax.all_to_all(
        intensity.reshape(run_count, 1, bin_count, local_mz),
        "freq",
        split_axis=2,
        concat_axis=1,
        tiled=True,
    ).astype(jnp.float32)
    raw_re = jnp.einsum("ap,kpim->kaim", cos_dev, samples, precision=PRECISE)
    raw_im = -jnp.einsum("ap,kpim->kaim", sin_dev, samples, precision=PRECISE)
    half_re = raw_re * twid_cos + raw_im * twid_sin
    half_im = raw_im * twid_cos - raw_re * twid_sin
    half_re, half_im = (half_re, half_im)
    piece_re = lax.all_to_all(half_re, "freq", split_axis=1, concat_axis=2, tiled=True)[:, 0]
    piece_im = lax.all_to_all(half_im, "freq", split_axis=1, concat_axis=2, tiled=True)[:, 0]
    out_re = jnp.einsum("bq,kqm->kbm", cos_bin, piece_re, precision=PRECISE) + jnp.einsum(
        "bq,kqm->kbm", sin_bin, piece_im, precision=PRECISE
    )
    out_im = jnp.einsum("bq,kqm->kbm", cos_bin, piece_im, precision=PRECISE) - jnp.einsum(
        "bq,kqm->kbm", sin_bin, piece_re, precision=PRECISE
    )
    model_re, model_im = own_model(loadings, shifts)
    numerator = (
        jnp.einsum("kbr,kbm->rm", weights_col * model_re, out_re, precision=PRECISE)
        + jnp.einsum("kbr,kbm->rm", weights_col * model_im, out_im, precision=PRECISE)
    ) * norm_scale
    run_share = run_count // mz_count
    run_amp = lax.dynamic_slice_in_dim(loadings, mz_rank * run_share, run_share, 0)
    run_lag = lax.dynamic_slice_in_dim(shifts, mz_rank * run_share, run_share, 0)
    model_re, model_im = own_model(run_amp, run_lag)
    gram_matrix = lax.psum(
        jnp.einsum("kbr,kbs->rs", weights_col * model_re, model_re, precision=PRECISE)
        + jnp.einsum("kbr,kbs->rs", weights_col * model_im, model_im, precision=PRECISE),
        ("freq", "mz"),
    )
    owned = lax.psum_scatter(numerator, "freq", scatter_dimension=1, tiled=True)
    return cholesky_solve(gram_matrix, owned)


def solution(mesh):
    in_specs = (P(None, "freq", "mz"), P(("freq", "mz"), None), P(), P(), P())
    out_specs = P(None, ("mz", "freq"))
    return jax.shard_map(
        on_device, mesh=mesh, in_specs=in_specs, out_specs=out_specs, check_vma=False
    )
```

profile of v0, /device:TPU:1, one launch (start us, length us, event | category | flops | bytes accessed | tf_op | source)
XLA Modules:
  0.0 1160.7 jit_solution(4711913364988517103)
XLA Ops:
  6.5 3.4 copy.76
  10.0 10.0 all-to-all-start
  20.0 0.1 fusion.179
  20.1 38.8 %all-to-all-done = bf16[8,1,192,512]{3,0,1,2:T(8,128)(2,1)S(1)} async-done(((bf16[8,1,192,512]{3,0,1,2:T(8,128)(2,1)}), bf16[8,1,192,512]{3,0,1,2:T(8,128)(2,1)S(1)}, u32[]{:S(2)}, u32[]{:S(2)}) %all-to-all-start) | async-done | bytes 1572896 | tf_op jit(solution)/shard_map/all_to_all | solution.py:70
  58.9 3.0 fusion.14
  61.9 5.3 subtract_bitcast_fusion
  67.1 3.5 copy.42
  70.7 4.4 all-to-all-start.1
  75.1 5.4 copy.44
  80.5 0.0 copy-start.2
  80.5 0.0 copy-start.4
  80.5 0.0 copy-start.3
  80.5 66.5 %all-to-all-done.1 = f32[8,32,6,512]{3,0,2,1:T(8,128)S(1)} async-done(((f32[8,32,6,512]{3,0,2,1:T(8,128)}), f32[8,32,6,512]{3,0,2,1:T(8,128)S(1)}, u32[]{:S(2)}, u32[]{:S(2)}) %all-to-all-start.1) | async-done | bytes 3145760 | tf_op jit(solution)/shard_map/all_to_all | solution.py:82
  147.0 5.5 all-to-all-start.2
  152.6 0.0 all-gather.2.cloned.1.call-start
  152.6 0.7 all-gather.2.cloned.1.call-update
  153.3 0.0 reduce-scatter.4.cloned.1.call-start
  153.3 0.0 copy-done.2
  153.4 0.1 reshape.152
  153.4 0.2 dynamic-slice_reduce_fusion
  153.6 0.0 copy-done.4
  153.7 0.0 copy-done.3
  153.7 0.1 fusion.204
  153.7 0.1 fusion.202
  153.8 719.5 %all-gather.2.cloned.1.call-done = f32[6144,64]{1,0:T(8,128)} async-done(((f32[24,64]{1,0:T(8,128)}), f32[6144,64]{1,0:T(8,128)}) %all-gather.2.cloned.1.call-update) | async-done | bytes 1572880 | tf_op jit(solution)/shard_map/all_gather | solution.py:43
  873.3 2.6 multiply_reduce_fusion
  875.9 1.1 fusion.88
  877.0 1.1 fusion.86
  878.1 1.1 fusion.33
  879.2 1.1 fusion.34
  880.3 0.8 fusion.96
  881.1 0.8 convolution_add_fusion.1
  881.9 79.3 %psum.7 = f32[64,64]{0,1:T(8,128)S(1)} all-reduce(f32[64,64]{0,1:T(8,128)S(1)} %convolution_add_fusion.1), channel_id=1, replica_groups=mesh['freq'=32,'mz'=8] {'freq','mz'}, use_global_device_ids=true, to_apply=%region_0.1 | all-reduce | flops 4096 | bytes 32768 | tf_op jit(solution)/shard_map/psum | solution.py:99
  961.3 0.1 copy.38
  961.4 5.8 cholesky.16
  967.2 7.3 fusion.12
  974.6 7.4 fusion.10
  982.0 0.0 all-to-all-done.2
  982.0 7.5 fusion.8
  989.5 0.0 copy-start.1
  989.5 7.7 fusion.6
  997.2 0.0 copy-done.1
  997.2 0.0 copy-start
  997.2 8.6 fusion.18
  1005.8 0.0 copy-done
  1005.8 9.4 fusion.30
  1015.2 0.0 reduce-scatter.4.cloned.1.call-update
  1015.2 0.6 compare_reduce_fusion
  1015.9 0.7 fusion.141
  1016.5 4.9 custom-call.8
  1021.4 130.3 %reduce-scatter.4.cloned.1.call-done = f32[16,64]{1,0:T(8,128)} async-done(((f32[512,64]{1,0:T(8,128)}), f32[16,64]{1,0:T(8,128)}) %reduce-scatter.4.cloned.1.call-update) | async-done | bytes 4112
  1151.8 0.8 fusion.144
  1152.6 0.8 fusion.142
  (6 shorter events, 0.1 us)
Async XLA Ops:
  10.0 48.9 %all-to-all-start = ((bf16[8,1,192,512]{3,0,1,2:T(8,128)(2,1)}), bf16[8,1,192,512]{3,0,1,2:T(8,128)(2,1)S(1)}, u32[]{:S(2)}, u32[]{:S(2)}) async-start(bf16[8,1,192,512]{3,0,1,2:T(8,128)(2,1)} %bitcast.79), calls=%async_computation | async-start | bytes 3145728 | tf_op jit(solution)/shard_map/all_to_all | solution.py:70
  70.7 76.4 %all-to-all-start.1 = ((f32[8,32,6,512]{3,0,2,1:T(8,128)}), f32[8,32,6,512]{3,0,2,1:T(8,128)S(1)}, u32[]{:S(2)}, u32[]{:S(2)}) async-start(f32[8,32,6,512]{3,0,2,1:T(8,128)} %copy.42), calls=%async_computation.1 | async-start | bytes 6291456 | tf_op jit(solution)/shard_map/all_to_all | solution.py:82
  80.5 72.9 %copy-start.2 = (f32[6144]{0:T(1024)S(1)}, f32[6144]{0:T(1024)}, u32[]{:S(2)}) copy-start(f32[6144]{0:T(1024)} %param.9) | copy-start | bytes 73732
  80.5 73.1 %copy-start.4 = (f32[8,64]{1,0:T(8,128)S(1)}, f32[8,64]{1,0:T(8,128)}, u32[]{:S(2)}) copy-start(f32[8,64]{1,0:T(8,128)} %param.7) | copy-start | bytes 6148
  80.5 73.2 %copy-start.3 = (s32[8,64]{1,0:T(8,128)S(1)}, s32[8,64]{1,0:T(8,128)}, u32[]{:S(2)}) copy-start(s32[8,64]{1,0:T(8,128)} %param.8) | copy-start | bytes 6148
  147.0 835.0 %all-to-all-start.2 = ((f32[8,32,6,512]{3,0,2,1:T(8,128)}), f32[8,32,6,512]{3,0,2,1:T(8,128)}, u32[]{:S(2)}, u32[]{:S(2)}) async-start(f32[8,32,6,512]{3,0,2,1:T(8,128)} %copy.44), calls=%async_computation.2 | async-start | bytes 6291456 | tf_op jit(solution)/shard_map/all_to_all | solution.py:83
  152.6 720.7 %all-gather.2.cloned.1.call-start = ((), (), s32[]{:S(2)}) async-start(), calls=%async_computation.4 | async-start | bytes 3158016 | tf_op jit(solution)/shard_map/all_gather | solution.py:43
  153.3 998.5 %reduce-scatter.4.cloned.1.call-start = ((), (), s32[]{:S(2)}) async-start(), calls=%async_computation.5 | async-start | bytes 270336
  989.5 7.7 copy-start.1
  997.2 8.7 copy-start
Sparse Core Ops, SparseCore 0:
  155.2 717.9 all-gather.1
  1015.4 136.3 reduce-scatter.3
where the time goes:
time: 1170 us; the launch traced here: 1160 us
  waiting for transfers between devices  956 us (82%)
  blocking collectives  79.3 us (7%)
  matrix products  63.8 us (5%)
  starting transfers between devices  20.1 us (2%)
  other arithmetic  14.9 us (1%)
  between operations  14.1 us (1%)
  local copies, waits for them, and re-layouts  12.7 us (1%)
    all_gather x1, waiting for transfers between devices, on_device(): full_elution = lax.all_gather(elution, ('freq', 'mz'), axis=0, tiled=True)  719 us
    unnamed x3, waiting for transfers between devices  131 us
    psum x1, blocking collectives, on_device(): lax.psum(jnp.einsum('kbr,kbs->rs', weights_col * model_re, model_re, prec...  79.3 us
    all_to_all x1, waiting for transfers between devices, on_device(): lax.all_to_all(half_re, 'freq', split_axis=1, concat_axis=2, tiled=True)  66.5 us
    all_to_all x1, waiting for transfers between devices, on_device(): lax.all_to_all(intensity.reshape(run_count, 1, bin_count, local_mz), 'fre...  38.8 us
  transfers between devices with their start and end apart: 5, of which 4 were waited for; matrix products, arithmetic and copies ran while one was open for 4% of the time, Pallas kernels for 0%

commit v1 on v0

v1 whole, which is shorter than its diff:
```python
import functools
import math

import jax
import jax.numpy as jnp
import numpy as np
from jax import lax
from jax.experimental import pallas as pl
from jax.experimental.pallas import tpu as pltpu
from jax.sharding import PartitionSpec as P

MESH = pl.DeviceIdType.MESH
HIGHEST = lax.Precision.HIGHEST
F32 = jnp.float32
BF16 = jnp.bfloat16

LENGTH = 6144
ROWS = 48
LANES = 128
RUNS = 8
COMP = 64
BLOCK = 192
CHANNELS = 512
FREQ = 32
OWN = 16
WINDOW = 512


def transform_tables():
    x48 = np.arange(ROWS)
    b128 = np.arange(LANES)
    inner = 2.0 * np.pi / ROWS * ((x48[:, None] * x48[None, :]) % ROWS)
    middle = 2.0 * np.pi / LENGTH * ((x48[:, None] * b128[None, :]) % LENGTH)
    outer = 2.0 * np.pi / LANES * ((b128[:, None] * b128[None, :]) % LANES)
    first = np.concatenate([np.cos(inner), np.sin(inner)], axis=0)
    turn = np.concatenate([np.cos(middle), np.sin(middle)], axis=0)
    last = np.concatenate([np.cos(outer), -np.sin(outer)], axis=0) / LENGTH
    return [jnp.asarray(t.astype(np.float32)) for t in (first, turn, last)]


def split(value):
    high = value.astype(BF16)
    low = (value - high.astype(F32)).astype(BF16)
    return high, low


def half_turn(value):
    return pltpu.roll(value, 64, 1)


def lag_weights(weight, first, turn, last, flip):
    inner = jnp.dot(first, weight, precision=HIGHEST, preferred_element_type=F32)
    cos_part, sin_part = inner[:ROWS], inner[ROWS:]
    tcos, tsin = turn[:ROWS], turn[ROWS:]
    real = cos_part * tcos - sin_part * tsin
    imag = cos_part * tsin + sin_part * tcos
    both = jnp.concatenate([real, imag], axis=1)
    by_x = jnp.dot(both, last, precision=HIGHEST, preferred_element_type=F32)
    padded = jnp.concatenate([by_x, jnp.zeros((LANES - ROWS, LANES), F32)], axis=0)
    flip[...] = jnp.transpose(padded)
    lane = lax.broadcasted_iota(jnp.int32, (16, LANES), 1)

    def part(index, shift):
        rows = flip[pl.ds(index, 16, stride=8), :]
        return rows if shift == 0 else pltpu.roll(rows, shift, 1)

    first_row = jnp.where(lane < 48, part(0, 0), jnp.where(lane < 96, part(1, 48), part(2, 96)))
    second_row = jnp.where(
        lane < 16, part(2, 96), jnp.where(lane < 64, part(3, 16), jnp.where(lane < 112, part(4, 64), part(5, 112)))
    )
    third_row = jnp.where(lane < 32, part(5, 112), jnp.where(lane < 80, part(6, 32), part(7, 80)))
    return first_row, second_row, third_row


def shifted(window, amount):
    value = window
    for bit in (128, 64, 32, 16, 8):
        rows = BLOCK + bit
        value = jnp.where((amount & bit) != 0, value[bit : bit + rows], value[0:rows])
    for bit in (4, 2, 1):
        value = jnp.where((amount & bit) != 0, pltpu.roll(value, value.shape[0] - bit, 0), value)
    return pltpu.roll(value, value.shape[0] - 1, 0)[0:BLOCK]


def kernel(
    elution_ref,
    loadings_ref,
    shifts_ref,
    weight_ref,
    first_ref,
    turn_ref,
    last_ref,
    intensity_ref,
    out_ref,
    samples,
    mine,
    theirs,
    blocks,
    profile,
    lags,
    flip,
    toeplitz,
    total,
    window,
    gram_send,
    gram_core,
    gram_x,
    gram_z,
    num_send,
    num_recv,
    load_sem,
    pair_sem,
    z_send,
    z_recv,
    p_send,
    p_recv,
    q_send,
    q_recv,
    swap_send,
    swap_recv,
    gram_sems,
    num_sems,
    num_recv_sems,
):
    freq = lax.axis_index("freq")
    mz = lax.axis_index("mz")
    core = freq % 2
    z_lo = (freq // 2) % 4
    x = freq // 8
    y = mz // 2
    z_hi = mz % 2
    p = x * (1 - core) + y * core
    q = y * (1 - core) + x * core

    def at(x_to, y_to, z_to, core_to):
        return (x_to * 8 + (z_to % 4) * 2 + core_to, y_to * 2 + z_to // 4)

    def at_pq(p_to, q_to):
        return at(p_to * (1 - core) + q_to * core, q_to * (1 - core) + p_to * core, z_hi * 4 + z_lo, core)

    partner = (freq + 1 - 2 * core, mz)
    z_mine = z_hi * 4 + z_lo

    barrier = pltpu.get_barrier_semaphore()

    def greet(step, carry):
        pl.semaphore_signal(barrier, inc=1, device_id=((freq + step) % FREQ, mz), device_id_type=MESH)
        return carry

    lax.fori_loop(1, FREQ, greet, 0)
    for step in range(1, 4):
        pl.semaphore_signal(
            barrier, inc=1, device_id=(freq, ((y + step) % 4) * 2 + z_hi), device_id_type=MESH
        )
    for step in range(4):
        pl.semaphore_signal(
            barrier, inc=1, device_id=at(x, y, (1 - z_hi) * 4 + step, core), device_id_type=MESH
        )

    load = pltpu.make_async_copy(intensity_ref, samples, load_sem)
    load.start()
    own_rows = elution_ref[...]
    mine[...] = jnp.concatenate([own_rows, own_rows], axis=1)

    lag_rows = lag_weights(weight_ref[...], first_ref[...], turn_ref[...], last_ref[...], flip)
    for z in range(3):
        lags[z] = lag_rows[z]

    pl.semaphore_wait(barrier, FREQ - 1 + 3 + 4)

    def remote(source, target, send, recv, device):
        return pltpu.make_async_remote_copy(
            src_ref=source, dst_ref=target, send_sem=send, recv_sem=recv, device_id=device, device_id_type=MESH
        )

    pair = remote(mine, theirs, pair_sem.at[0], pair_sem.at[1], partner)
    pair.start()
    pair.wait()
    lane24 = lax.broadcasted_iota(jnp.int32, (24, LANES), 1)
    side = (lane24 // 64) == core
    z_copies = []
    for step in range(1, 8):
        z_to = (z_mine + step) % 8
        z_copies.append(
            remote(
                blocks.at[core, q, p, z_lo],
                blocks.at[core, q, p, z_lo],
                z_send.at[step - 1],
                z_recv.at[z_lo],
                at(x, y, z_to, core),
            )
        )

    @pl.when(z_hi == core)
    def _():
        blocks[core, q, p, z_lo] = jnp.where(side, mine[...], theirs[...])
        for copy in z_copies:
            copy.start()

    row = lax.broadcasted_iota(jnp.int32, (LANES, LANES), 0)
    lane = lax.broadcasted_iota(jnp.int32, (LANES, LANES), 1)
    upper = lane >= row

    def turned(z, g):
        base = jnp.broadcast_to(lags[z, pl.ds(g, 1), :], (LANES, LANES))
        return pltpu.roll(base, 0, 1, stride=1, stride_axis=0)

    def build(g, before):
        for z in range(3):
            here = turned(z, g)
            high, low = split(jnp.where(upper, here, before))
            toeplitz[0, 3 * g + z] = high
            toeplitz[1, 3 * g + z] = low
            before = here
        return before

    lax.fori_loop(0, 16, build, turned(2, 15))

    for source in range(4):

        @pl.when(jnp.logical_or(z_hi != core, z_lo != source))
        def _(source=source):
            spot = blocks.at[core, q, p, source]
            remote(spot, spot, z_send.at[0], z_recv.at[source], partner).wait_recv()

    swaps = [remote(blocks.at[core, q, p], blocks.at[core, q, p], swap_send.at[0], swap_recv.at[0], partner)]
    swaps[0].start()
    p_copies = []
    for step in range(1, 4):
        copy = remote(
            blocks.at[core, q, p],
            blocks.at[core, q, p],
            p_send.at[step - 1],
            p_recv.at[step - 1],
            at_pq((p + step) % 4, q),
        )
        copy.start()
        p_copies.append(copy)
    for step in range(1, 4):
        spot = blocks.at[core, q, (p + 4 - step) % 4]
        remote(spot, spot, p_send.at[step - 1], p_recv.at[step - 1], partner).wait_recv()
        swap = remote(spot, spot, swap_send.at[step], swap_recv.at[step], partner)
        swap.start()
        swaps.append(swap)
    q_copies = []
    for step in range(1, 4):
        copy = remote(
            blocks.at[core, q], blocks.at[core, q], q_send.at[step - 1], q_recv.at[step - 1], at_pq(p, (q + step) % 4)
        )
        copy.start()
        q_copies.append(copy)
    for step in range(1, 4):
        spot = blocks.at[core, (q + 4 - step) % 4]
        remote(spot, spot, q_send.at[step - 1], q_recv.at[step - 1], partner).wait_recv()
        swap = remote(spot, spot, swap_send.at[3 + step], swap_recv.at[3 + step], partner)
        swap.start()
        swaps.append(swap)
    other = 1 - core
    spot = blocks.at[other, p, q]
    remote(spot, spot, swap_send.at[0], swap_recv.at[0], partner).wait_recv()
    for step in range(1, 4):
        spot = blocks.at[other, p, (q + 4 - step) % 4]
        remote(spot, spot, swap_send.at[step], swap_recv.at[step], partner).wait_recv()
    for step in range(1, 4):
        spot = blocks.at[other, (p + 4 - step) % 4]
        remote(spot, spot, swap_send.at[3 + step], swap_recv.at[3 + step], partner).wait_recv()

    left = lax.broadcasted_iota(jnp.int32, (24, LANES), 1) < 64

    def unpack(index, carry):
        x_at = index // 4
        zl_at = index % 4
        low_rows, high_rows = [], []
        for y_at in range(4):
            for zh_at in range(2):
                if zh_at == 0:
                    block = blocks[0, y_at, x_at, zl_at]
                else:
                    block = blocks[1, x_at, y_at, zl_at]
                rounded = block.astype(BF16).astype(F32)
                rest = block - rounded
                low_rows.append(jnp.where(left, rounded, half_turn(rest)))
                high_rows.append(jnp.where(left, half_turn(rounded), rest))
        start = pl.multiple_of(index * 384, 128)
        profile[pl.ds(start, BLOCK), :] = jnp.concatenate(low_rows, axis=0).astype(BF16)
        profile[pl.ds(start + BLOCK, BLOCK), :] = jnp.concatenate(high_rows, axis=0).astype(BF16)
        return carry

    lax.fori_loop(0, 16, unpack, 0)
    profile[LENGTH : LENGTH + WINDOW, :] = profile[0:WINDOW, :]

    begin = ((freq * 3 + 96 - 4) // 2) % ROWS
    total[...] = jnp.zeros_like(total)

    def filtered(tile, carry):
        pieces = []
        for part in range(2):
            for row_block in (0, 2):
                spot = 2 * tile + 2 * ROWS - begin - row_block
                pieces.append(
                    jnp.concatenate([toeplitz[part, spot % ROWS], toeplitz[part, (spot + 1) % ROWS]], axis=1)
                )
        start = pl.multiple_of(tile * 256, 128)
        rows = jnp.concatenate([profile[pl.ds(start, 256), :], profile[pl.ds(start + 128, 256), :]], axis=1)
        total[...] += jnp.dot(jnp.concatenate(pieces, axis=0), rows, preferred_element_type=F32)
        return carry

    lax.fori_loop(0, 24, filtered, 0)
    for row_block in range(4):
        base = (row_block // 2) * 128
        cut = pl.ds((row_block % 2) * 128, 128)
        value = total[pl.ds(base, 128), cut] + total[pl.ds(256 + base, 128), cut]
        window[0, pl.ds(row_block * 128, 128), :] = value + half_turn(value)
        start = pl.multiple_of(begin * 128 + row_block * 128, 128)
        value = profile[pl.ds(start, 128), :].astype(F32)
        window[1, pl.ds(row_block * 128, 128), :] = value + half_turn(value)

    skip = pl.multiple_of((freq % 2) * 64, 64)
    load.wait()
    filtered_rows = window[0, pl.ds(skip, 448), :]
    plain_rows = window[1, pl.ds(skip, 448), :]
    quad = jnp.zeros((256, 256), F32)
    numer = jnp.zeros((COMP, CHANNELS), F32)
    stacks = []
    for pair_at in range(RUNS // 2):
        amount = jnp.concatenate([shifts_ref[2 * pair_at : 2 * pair_at + 1], shifts_ref[2 * pair_at + 1 : 2 * pair_at + 2]], axis=1)
        gain = jnp.concatenate(
            [loadings_ref[2 * pair_at : 2 * pair_at + 1], loadings_ref[2 * pair_at + 1 : 2 * pair_at + 2]], axis=1
        )
        moved = jnp.transpose(shifted(filtered_rows, 255 - amount) * gain)
        model_high, model_low = split(shifted(plain_rows, 255 - amount) * gain)
        high, low = split(moved)
        stacks.append((high, low))
        quad = quad + jnp.dot(
            jnp.concatenate([high, low], axis=0),
            jnp.concatenate([model_high, model_low], axis=1),
            preferred_element_type=F32,
        )
    corner = quad[:128, :128] + quad[:128, 128:] + quad[128:, :128]
    gram_own = corner[:64] + half_turn(corner[64:])
    left32 = lax.broadcasted_iota(jnp.int32, (32, LANES), 1) < 64
    gram_send[0] = jnp.where(left32, gram_own[:32], half_turn(gram_own[32:]))
    core_copy = remote(gram_send.at[0], gram_core, gram_sems.at[0], gram_sems.at[1], partner)
    core_copy.start()

    for run in range(RUNS):
        high, low = stacks[run // 2]
        cut = slice((run % 2) * 64, (run % 2) * 64 + 64)
        both = jnp.dot(
            jnp.concatenate([high[cut], low[cut]], axis=0), samples[run], preferred_element_type=F32
        )
        numer = numer + both[:64] + both[64:]
    by_channel = jnp.transpose(numer).reshape(FREQ, 2, 8, COMP)
    num_send[...] = jnp.concatenate([by_channel[:, 0], by_channel[:, 1]], axis=2)

    def num_copy(step):
        to = (freq + step) % FREQ
        return remote(num_send.at[to], num_recv.at[freq], num_sems.at[step], num_recv_sems.at[step], (to, mz))

    def send_num(step, carry):
        num_copy(step).start()
        return carry

    core_copy.wait()
    gram_send[1] = gram_send[0] + gram_core[...]
    x_copies = []
    for step in range(1, 4):
        copy = remote(
            gram_send.at[1],
            gram_x.at[step - 1],
            gram_sems.at[1 + step],
            gram_sems.at[4 + step],
            at((x + step) % 4, y, z_mine, core),
        )
        copy.start()
        x_copies.append(copy)
    lax.fori_loop(1, FREQ, send_num, 0)
    for copy in x_copies:
        copy.wait()
    gram_send[2] = (gram_send[1] + gram_x[0]) + (gram_x[1] + gram_x[2])
    z_grams = []
    for step in range(1, 4):
        copy = remote(
            gram_send.at[2],
            gram_z.at[step - 1],
            gram_sems.at[7 + step],
            gram_sems.at[10 + step],
            at(x, y, z_hi * 4 + (z_lo + step) % 4, core),
        )
        copy.start()
        z_grams.append(copy)
    for copy in z_grams:
        copy.wait()
    packed = (gram_send[2] + gram_z[0]) + (gram_z[1] + gram_z[2])

    row64 = lax.broadcasted_iota(jnp.int32, (COMP, LANES), 0)
    lane64 = lax.broadcasted_iota(jnp.int32, (COMP, LANES), 1)
    unit = (lane64 == row64 + COMP).astype(F32)
    matrix = jnp.where(lane64 < COMP, jnp.concatenate([packed, half_turn(packed)], axis=0), unit)
    for step in range(COMP):
        pivot = matrix[step : step + 1, :]
        scaled = pivot * (1.0 / matrix[step : step + 1, step : step + 1])
        matrix = jnp.where(row64 == step, scaled, matrix - matrix[:, step : step + 1] * scaled)
    inverse = matrix[:, COMP:]

    def wait_num(step, carry):
        source = (freq + FREQ - step) % FREQ
        copy = remote(num_send.at[source], num_recv.at[source], num_sems.at[step], num_recv_sems.at[step], (source, mz))
        copy.wait_recv()
        return carry

    lax.fori_loop(1, FREQ, wait_num, 0)
    num_recv[freq] = num_send[freq]
    summed = jnp.sum(num_recv[...], axis=0)
    own_channels = jnp.concatenate([summed[:, :64], summed[:, 64:]], axis=0)
    out_ref[...] = lax.dot_general(
        inverse, own_channels, (((1,), (1,)), ((), ())), precision=HIGHEST, preferred_element_type=F32
    )

    @pl.when(z_hi == core)
    def _():
        for copy in z_copies:
            copy.wait_send()

    for copy in p_copies + q_copies + swaps:
        copy.wait_send()

    def drain(step, carry):
        num_copy(step).wait_send()
        return carry

    lax.fori_loop(1, FREQ, drain, 0)


def on_device(intensity, elution, loadings, shifts, bin_weight):
    first, turn, last = transform_tables()
    vmem = pl.BlockSpec(memory_space=pltpu.VMEM)
    dma = pltpu.SemaphoreType.DMA
    return pl.pallas_call(
        kernel,
        out_shape=jax.ShapeDtypeStruct((COMP, OWN), F32),
        in_specs=[vmem] * 7 + [pl.BlockSpec(memory_space=pl.ANY)],
        out_specs=vmem,
        scratch_shapes=[
            pltpu.VMEM((RUNS, BLOCK, CHANNELS), BF16),
            pltpu.VMEM((24, LANES), F32),
            pltpu.VMEM((24, LANES), F32),
            pltpu.VMEM((2, 4, 4, 4, 24, LANES), F32),
            pltpu.VMEM((LENGTH + WINDOW, LANES), BF16),
            pltpu.VMEM((3, 16, LANES), F32),
            pltpu.VMEM((LANES, LANES), F32),
            pltpu.VMEM((2, ROWS, LANES, LANES), BF16),
            pltpu.VMEM((512, 256), F32),
            pltpu.VMEM((2, WINDOW, LANES), F32),
            pltpu.VMEM((3, 32, LANES), F32),
            pltpu.VMEM((32, LANES), F32),
            pltpu.VMEM((3, 32, LANES), F32),
            pltpu.VMEM((3, 32, LANES), F32),
            pltpu.VMEM((FREQ, 8, LANES), F32),
            pltpu.VMEM((FREQ, 8, LANES), F32),
            dma,
            dma((2,)),
            dma((7,)),
            dma((4,)),
            dma((3,)),
            dma((3,)),
            dma((3,)),
            dma((3,)),
            dma((7,)),
            dma((7,)),
            dma((14,)),
            dma((FREQ,)),
            dma((FREQ,)),
        ],
        compiler_params=pltpu.CompilerParams(
            collective_id=0, has_side_effects=True, vmem_limit_bytes=48 * 1024 * 1024
        ),
    )(elution, loadings, shifts, bin_weight.reshape(ROWS, LANES), first, turn, last, intensity)


def solution(mesh):
    in_specs = (P(None, "freq", "mz"), P(("freq", "mz"), None), P(), P(), P())
    out_specs = P(None, ("mz", "freq"))
    return jax.shard_map(on_device, mesh=mesh, in_specs=in_specs, out_specs=out_specs, check_vma=False)
```

time: 1170 us -> 59.3 us (0.05)
  waiting for transfers between devices: 956 us -> 0 us
  blocking collectives: 79.3 us -> 0 us
  matrix products: 63.8 us -> 0 us
  Pallas kernels: 0 us -> 51.4 us
  starting transfers between devices: 20.1 us -> 0 us
  other arithmetic: 14.9 us -> 0 us
  between operations: 14.1 us -> 0.02 us
    all_gather x1 -> x0, waiting for transfers between devices: 719 us -> none  [on_device(): full_elution = lax.all_gather(elution, ('freq', 'mz'), axis=0, tiled=True)]
    unnamed x3 -> x0, waiting for transfers between devices: 131 us -> none
    all_to_all x3 -> x0, waiting for transfers between devices: 105 us -> none  [the longest x1 66.5 us: on_device(): lax.all_to_all(half_re, 'freq', split_axis=1, concat_axis=2, tiled=True)]
    psum x1 -> x0, blocking collectives: 79.3 us -> none  [on_device(): lax.psum(jnp.einsum('kbr,kbs->rs', weights_col * model_re, model_re, prec...]
    dot_general x14 -> x0, matrix products: 62.2 us -> none  [the longest x1 9.39 us: on_device(): jnp.einsum('kbr,kbm->rm', weights_col * model_im, out_im, precision=PRECISE)]
    pallas_call x0 -> x1, Pallas kernels: none -> 51.4 us  [on_device(): pl.pallas_call(kernel, out_shape=jax.ShapeDtypeStruct((COMP, OWN), F32),...]
    all_to_all x3 -> x0, starting transfers between devices: 20 us -> none  [the longest x1 10 us: on_device(): lax.all_to_all(intensity.reshape(run_count, 1, bin_count, local_mz), 'fre...]
    another operation x5 -> x0, other arithmetic: 12.1 us -> none  [the longest x3 6.51 us: cholesky_solve(): factor = jnp.linalg.cholesky(gram_matrix)]
  transfers between devices with their start and end apart: 5 -> 0, of which waited for: 4 -> 0; matrix products, arithmetic and copies ran while one was open for 4% -> 0% of each run, Pallas kernels for 0% -> 0%
where the time goes in v1:
time: 59.3 us; the launch traced here: 58.9 us
  Pallas kernels  51.4 us (87%)
  local copies, waits for them, and re-layouts  7.39 us (12%)
    pallas_call x1, Pallas kernels, on_device(): pl.pallas_call(kernel, out_shape=jax.ShapeDtypeStruct((COMP, OWN), F32),...  51.4 us
    unnamed x16, local copies, waits for them, and re-layouts  6.72 us

profile of v1, /device:TPU:1, one launch (start us, length us, event | category | flops | bytes accessed | tf_op | source)
XLA Modules:
  0.0 58.9 jit_solution(9120111233373161616)
XLA Ops:
  0.0 0.0 copy-start
  0.0 1.4 %copy-done = bf16[8,192,512]{2,1,0:T(8,128)(2,1)S(1)} copy-done((bf16[8,192,512]{2,1,0:T(8,128)(2,1)S(1)}, bf16[8,192,512]{2,1,0:T(8,128)(2,1)}, u32[]{:S(2)}) %copy-start) | copy-done | bytes 1572888
  1.4 0.0 copy-start.1
  1.4 0.9 %copy-done.1 = f32[256,128]{1,0:T(8,128)S(1)} copy-done((f32[256,128]{1,0:T(8,128)S(1)}, f32[256,128]{1,0:T(8,128)}, u32[]{:S(2)}) %copy-start.1) | copy-done | bytes 131096
  2.3 0.0 copy-start.2
  2.3 0.8 %copy-done.2 = f32[96,128]{1,0:T(8,128)S(1)} copy-done((f32[96,128]{1,0:T(8,128)S(1)}, f32[96,128]{1,0:T(8,128)}, u32[]{:S(2)}) %copy-start.2) | copy-done | bytes 49176
  3.1 0.0 copy-start.3
  3.1 0.8 %copy-done.3 = f32[96,48]{1,0:T(8,128)S(1)} copy-done((f32[96,48]{1,0:T(8,128)S(1)}, f32[96,48]{1,0:T(8,128)}, u32[]{:S(2)}) %copy-start.3) | copy-done | bytes 18456
  3.9 0.0 copy-start.4
  3.9 0.7 %copy-done.4 = f32[6144]{0:T(1024)S(1)} copy-done((f32[6144]{0:T(1024)S(1)}, f32[6144]{0:T(1024)}, u32[]{:S(2)}) %copy-start.4) | copy-done | bytes 24600
  4.6 0.0 copy-start.5
  4.7 0.7 %copy-done.5 = f32[24,64]{1,0:T(8,128)S(1)} copy-done((f32[24,64]{1,0:T(8,128)S(1)}, f32[24,64]{1,0:T(8,128)}, u32[]{:S(2)}) %copy-start.5) | copy-done | bytes 6168
  5.4 0.0 copy-start.6
  5.4 0.7 %copy-done.6 = f32[8,64]{1,0:T(8,128)S(1)} copy-done((f32[8,64]{1,0:T(8,128)S(1)}, f32[8,64]{1,0:T(8,128)}, u32[]{:S(2)}) %copy-start.6) | copy-done | bytes 2072
  6.0 0.0 copy-start.7
  6.0 0.7 %copy-done.7 = s32[8,64]{1,0:T(8,128)S(1)} copy-done((s32[8,64]{1,0:T(8,128)S(1)}, s32[8,64]{1,0:T(8,128)}, u32[]{:S(2)}) %copy-start.7) | copy-done | bytes 2072
  6.7 51.4 %shard_map.82 = f32[64,16]{1,0:T(8,128)S(1)} custom-call(f32[24,64]{1,0:T(8,128)S(1)} %copy-done.5, f32[8,64]{1,0:T(8,128)S(1)} %copy-done.6, s32[8,64]{1,0:T(8,128)S(1)} %copy-done.7, f32[48,128]{1,0:T(8,128)S(1)} %bitcast.1, f32[96,48]{1,0:T(8,128)S(1)} %copy-done.3, f32[96,128]{1,0:T(8,128)S(1)} %copy-done.2, f32[256,128]{1,0:T(8,128)S(1)} %copy-done.1, ...), custom_call_target="tpu_custom_call" | custom-call | tf_op jit(solution)/shard_map/pallas_call | solution.py:439
  58.2 0.7 %copy.9 = f32[64,16]{0,1:T(8,128)} copy(f32[64,16]{1,0:T(8,128)S(1)} %shard_map.82) | data formatting | bytes 8192 | tf_op jit(solution)/shard_map/pallas_call | solution.py:439
Async XLA Ops:
  0.0 1.4 %copy-start = (bf16[8,192,512]{2,1,0:T(8,128)(2,1)S(1)}, bf16[8,192,512]{2,1,0:T(8,128)(2,1)}, u32[]{:S(2)}) copy-start(bf16[8,192,512]{2,1,0:T(8,128)(2,1)} %intensity_ref.1) | copy-start | bytes 4718596
  1.4 0.9 %copy-start.1 = (f32[256,128]{1,0:T(8,128)S(1)}, f32[256,128]{1,0:T(8,128)}, u32[]{:S(2)}) copy-start(f32[256,128]{1,0:T(8,128)} %constant.8.clone.last_ref) | copy-start | bytes 393220
  2.3 0.8 %copy-start.2 = (f32[96,128]{1,0:T(8,128)S(1)}, f32[96,128]{1,0:T(8,128)}, u32[]{:S(2)}) copy-start(f32[96,128]{1,0:T(8,128)} %constant.7.clone.turn_ref) | copy-start | bytes 147460
  3.1 0.8 %copy-start.3 = (f32[96,48]{1,0:T(8,128)S(1)}, f32[96,48]{1,0:T(8,128)}, u32[]{:S(2)}) copy-start(f32[96,48]{1,0:T(8,128)} %constant.6.clone.first_ref) | copy-start | bytes 55300
  3.9 0.7 %copy-start.4 = (f32[6144]{0:T(1024)S(1)}, f32[6144]{0:T(1024)}, u32[]{:S(2)}) copy-start(f32[6144]{0:T(1024)} %param.12) | copy-start | bytes 73732
  4.6 0.7 %copy-start.5 = (f32[24,64]{1,0:T(8,128)S(1)}, f32[24,64]{1,0:T(8,128)}, u32[]{:S(2)}) copy-start(f32[24,64]{1,0:T(8,128)} %elution_ref.1) | copy-start | bytes 18436
  5.4 0.7 %copy-start.6 = (f32[8,64]{1,0:T(8,128)S(1)}, f32[8,64]{1,0:T(8,128)}, u32[]{:S(2)}) copy-start(f32[8,64]{1,0:T(8,128)} %loadings_ref.1) | copy-start | bytes 6148
  6.0 0.7 %copy-start.7 = (s32[8,64]{1,0:T(8,128)S(1)}, s32[8,64]{1,0:T(8,128)}, u32[]{:S(2)}) copy-start(s32[8,64]{1,0:T(8,128)} %shifts_ref.1) | copy-start | bytes 6148

commit v2 on v1

--- a/solution.py
+++ b/solution.py
@@ -33,9 +33,10 @@
     middle = 2.0 * np.pi / LENGTH * ((x48[:, None] * b128[None, :]) % LENGTH)
     outer = 2.0 * np.pi / LANES * ((b128[:, None] * b128[None, :]) % LANES)
     first = np.concatenate([np.cos(inner), np.sin(inner)], axis=0)
+    first = np.pad(first, ((0, 0), (0, LANES - ROWS)))
     turn = np.concatenate([np.cos(middle), np.sin(middle)], axis=0)
     last = np.concatenate([np.cos(outer), -np.sin(outer)], axis=0) / LENGTH
-    return [jnp.asarray(t.astype(np.float32)) for t in (first, turn, last)]
+    return jnp.asarray(np.concatenate([first, turn, last], axis=0).astype(np.float32))
 
 
 def split(value):
@@ -83,15 +84,18 @@
 
 
 def kernel(
+    elution_hbm,
+    loadings_hbm,
+    shifts_hbm,
+    weight_hbm,
+    tables_hbm,
+    intensity_hbm,
+    out_ref,
     elution_ref,
     loadings_ref,
     shifts_ref,
     weight_ref,
-    first_ref,
-    turn_ref,
-    last_ref,
-    intensity_ref,
-    out_ref,
+    tables_ref,
     samples,
     mine,
     theirs,
@@ -108,7 +112,7 @@
     gram_z,
     num_send,
     num_recv,
-    load_sem,
+    load_sems,
     pair_sem,
     z_send,
     z_recv,
@@ -141,6 +145,21 @@
     partner = (freq + 1 - 2 * core, mz)
     z_mine = z_hi * 4 + z_lo
 
+    loads = [
+        pltpu.make_async_copy(source, target, load_sems.at[index])
+        for index, (source, target) in enumerate(
+            (
+                (elution_hbm, elution_ref),
+                (weight_hbm, weight_ref),
+                (tables_hbm, tables_ref),
+                (loadings_hbm, loadings_ref),
+                (shifts_hbm, shifts_ref),
+                (intensity_hbm, samples),
+            )
+        )
+    ]
+    for load in loads:
+        load.start()
     barrier = pltpu.get_barrier_semaphore()
 
     def greet(step, carry):
@@ -157,12 +176,15 @@
             barrier, inc=1, device_id=at(x, y, (1 - z_hi) * 4 + step, core), device_id_type=MESH
         )
 
-    load = pltpu.make_async_copy(intensity_ref, samples, load_sem)
-    load.start()
+    loads[0].wait()
     own_rows = elution_ref[...]
     mine[...] = jnp.concatenate([own_rows, own_rows], axis=1)
 
-    lag_rows = lag_weights(weight_ref[...], first_ref[...], turn_ref[...], last_ref[...], flip)
+    loads[1].wait()
+    loads[2].wait()
+    lag_rows = lag_weights(
+        weight_ref[...], tables_ref[:96, :ROWS], tables_ref[96:192], tables_ref[192:448], flip
+    )
     for z in range(3):
         lags[z] = lag_rows[z]
 
@@ -316,7 +338,8 @@
         window[1, pl.ds(row_block * 128, 128), :] = value + half_turn(value)
 
     skip = pl.multiple_of((freq % 2) * 64, 64)
-    load.wait()
+    for load in loads[3:]:
+        load.wait()
     filtered_rows = window[0, pl.ds(skip, 448), :]
     plain_rows = window[1, pl.ds(skip, 448), :]
     quad = jnp.zeros((256, 256), F32)
@@ -374,7 +397,6 @@
         )
         copy.start()
         x_copies.append(copy)
-    lax.fori_loop(1, FREQ, send_num, 0)
     for copy in x_copies:
         copy.wait()
     gram_send[2] = (gram_send[1] + gram_x[0]) + (gram_x[1] + gram_x[2])
@@ -389,6 +411,7 @@
         )
         copy.start()
         z_grams.append(copy)
+    lax.fori_loop(1, FREQ, send_num, 0)
     for copy in z_grams:
         copy.wait()
     packed = (gram_send[2] + gram_z[0]) + (gram_z[1] + gram_z[2])
@@ -397,10 +420,17 @@
     lane64 = lax.broadcasted_iota(jnp.int32, (COMP, LANES), 1)
     unit = (lane64 == row64 + COMP).astype(F32)
     matrix = jnp.where(lane64 < COMP, jnp.concatenate([packed, half_turn(packed)], axis=0), unit)
-    for step in range(COMP):
-        pivot = matrix[step : step + 1, :]
-        scaled = pivot * (1.0 / matrix[step : step + 1, step : step + 1])
-        matrix = jnp.where(row64 == step, scaled, matrix - matrix[:, step : step + 1] * scaled)
+    for step in range(0, COMP, 2):
+        one = jnp.broadcast_to(matrix[:, step : step + 1], matrix.shape)
+        two = jnp.broadcast_to(matrix[:, step + 1 : step + 2], matrix.shape)
+        top, low = matrix[step : step + 1], matrix[step + 1 : step + 2]
+        one_top, one_low = one[step : step + 1], one[step + 1 : step + 2]
+        two_top, two_low = two[step : step + 1], two[step + 1 : step + 2]
+        scale = 1.0 / (one_top * two_low - two_top * one_low)
+        top_new = (two_low * top - two_top * low) * scale
+        low_new = (one_top * low - one_low * top) * scale
+        rest = matrix - one * top_new - two * low_new
+        matrix = jnp.where(row64 == step, top_new, jnp.where(row64 == step + 1, low_new, rest))
     inverse = matrix[:, COMP:]
 
     def wait_num(step, carry):
@@ -414,7 +444,7 @@
     summed = jnp.sum(num_recv[...], axis=0)
     own_channels = jnp.concatenate([summed[:, :64], summed[:, 64:]], axis=0)
     out_ref[...] = lax.dot_general(
-        inverse, own_channels, (((1,), (1,)), ((), ())), precision=HIGHEST, preferred_element_type=F32
+        own_channels, inverse, (((1,), (1,)), ((), ())), precision=HIGHEST, preferred_element_type=F32
     )
 
     @pl.when(z_hi == core)
@@ -433,15 +463,19 @@
 
 
 def on_device(intensity, elution, loadings, shifts, bin_weight):
-    first, turn, last = transform_tables()
     vmem = pl.BlockSpec(memory_space=pltpu.VMEM)
     dma = pltpu.SemaphoreType.DMA
-    return pl.pallas_call(
+    by_channel = pl.pallas_call(
         kernel,
-        out_shape=jax.ShapeDtypeStruct((COMP, OWN), F32),
-        in_specs=[vmem] * 7 + [pl.BlockSpec(memory_space=pl.ANY)],
+        out_shape=jax.ShapeDtypeStruct((OWN, COMP), F32),
+        in_specs=[pl.BlockSpec(memory_space=pltpu.HBM)] * 6,
         out_specs=vmem,
         scratch_shapes=[
+            pltpu.VMEM((24, COMP), F32),
+            pltpu.VMEM((RUNS, COMP), F32),
+            pltpu.VMEM((RUNS, COMP), jnp.int32),
+            pltpu.VMEM((ROWS, LANES), F32),
+            pltpu.VMEM((448, LANES), F32),
             pltpu.VMEM((RUNS, BLOCK, CHANNELS), BF16),
             pltpu.VMEM((24, LANES), F32),
             pltpu.VMEM((24, LANES), F32),
@@ -458,7 +492,7 @@
             pltpu.VMEM((3, 32, LANES), F32),
             pltpu.VMEM((FREQ, 8, LANES), F32),
             pltpu.VMEM((FREQ, 8, LANES), F32),
-            dma,
+            dma((6,)),
             dma((2,)),
             dma((7,)),
             dma((4,)),
@@ -473,9 +507,10 @@
             dma((FREQ,)),
         ],
         compiler_params=pltpu.CompilerParams(
-            collective_id=0, has_side_effects=True, vmem_limit_bytes=48 * 1024 * 1024
+            collective_id=0, has_side_effects=True, vmem_limit_bytes=67043328
         ),
-    )(elution, loadings, shifts, bin_weight.reshape(ROWS, LANES), first, turn, last, intensity)
+    )(elution, loadings, shifts, bin_weight.reshape(ROWS, LANES), transform_tables(), intensity)
+    return by_channel.T
 
 
 def solution(mesh):

time: 59.3 us -> 52.8 us (0.89)
  local copies, waits for them, and re-layouts: 7.39 us -> 1.3 us
    unnamed x16 -> x1, local copies, waits for them, and re-layouts: 6.72 us -> 1.3 us
    pallas_call x1 -> x0, local copies, waits for them, and re-layouts: 0.67 us -> none  [on_device(): pl.pallas_call(kernel, out_shape=jax.ShapeDtypeStruct((COMP, OWN), F32),...]
where the time goes in v2:
time: 52.8 us; the launch traced here: 52.6 us
  Pallas kernels  51.3 us (97%)
  local copies, waits for them, and re-layouts  1.3 us (2%)
    pallas_call x1, Pallas kernels, on_device(): pl.pallas_call(kernel, out_shape=jax.ShapeDtypeStruct((OWN, COMP), F32),...  51.3 us
    unnamed x1, local copies, waits for them, and re-layouts  1.3 us

profile of v2, /device:TPU:1, one launch (start us, length us, event | category | flops | bytes accessed | tf_op | source)
XLA Modules:
  0.0 52.6 jit_solution(14143923637204690922)
XLA Ops:
  0.0 51.3 %shard_map.64 = f32[16,64]{1,0:T(8,128)} custom-call(f32[24,64]{1,0:T(8,128)} %elution_hbm.1, f32[8,64]{1,0:T(8,128)} %loadings_hbm.1, s32[8,64]{1,0:T(8,128)} %shifts_hbm.1, f32[48,128]{1,0:T(8,128)} %bitcast.3, f32[448,128]{1,0:T(8,128)} %constant.2.clone.tables_hbm, bf16[8,192,512]{2,1,0:T(8,128)(2,1)} %intensity_hbm.1), custom_call_target="tpu_custom_call" | custom-call | tf_op jit(solution)/shard_map/pallas_call | solution.py:468
  51.3 1.3 %copy.8 = f32[64,16]{0,1:T(8,128)} copy(f32[64,16]{0,1:T(8,128)} %bitcast.2) | data formatting | bytes 8192

commit v3 on v2

--- a/solution.py
+++ b/solution.py
@@ -23,6 +23,7 @@
 CHANNELS = 512
 FREQ = 32
 OWN = 16
+SLAB = 1536
 WINDOW = 512
 
 
@@ -101,6 +102,7 @@
     theirs,
     blocks,
     profile,
+    slab,
     lags,
     flip,
     toeplitz,
@@ -116,10 +118,9 @@
     pair_sem,
     z_send,
     z_recv,
-    p_send,
-    p_recv,
-    q_send,
-    q_recv,
+    second_send,
+    third_send,
+    own_recv,
     swap_send,
     swap_recv,
     gram_sems,
@@ -202,20 +203,13 @@
     side = (lane24 // 64) == core
     z_copies = []
     for step in range(1, 8):
+        own = blocks.at[core, x, y, z_lo]
         z_to = (z_mine + step) % 8
-        z_copies.append(
-            remote(
-                blocks.at[core, q, p, z_lo],
-                blocks.at[core, q, p, z_lo],
-                z_send.at[step - 1],
-                z_recv.at[z_lo],
-                at(x, y, z_to, core),
-            )
-        )
+        z_copies.append(remote(own, own, z_send.at[step - 1], z_recv.at[z_lo], at(x, y, z_to, core)))
 
     @pl.when(z_hi == core)
     def _():
-        blocks[core, q, p, z_lo] = jnp.where(side, mine[...], theirs[...])
+        blocks[core, x, y, z_lo] = jnp.where(side, mine[...], theirs[...])
         for copy in z_copies:
             copy.start()
 
@@ -242,98 +236,131 @@
 
         @pl.when(jnp.logical_or(z_hi != core, z_lo != source))
         def _(source=source):
-            spot = blocks.at[core, q, p, source]
+            spot = blocks.at[core, x, y, source]
             remote(spot, spot, z_send.at[0], z_recv.at[source], partner).wait_recv()
 
-    swaps = [remote(blocks.at[core, q, p], blocks.at[core, q, p], swap_send.at[0], swap_recv.at[0], partner)]
-    swaps[0].start()
-    p_copies = []
-    for step in range(1, 4):
-        copy = remote(
-            blocks.at[core, q, p],
-            blocks.at[core, q, p],
-            p_send.at[step - 1],
-            p_recv.at[step - 1],
-            at_pq((p + step) % 4, q),
-        )
+    def offsets(a, b):
+        return (a * (1 - core) + b * core, b * (1 - core) + a * core)
+
+    def piece(colour, dx, dy):
+        return blocks.at[colour, (x + dx) % 4, (y + dy) % 4]
+
+    sent = []
+
+    def begin_copy(source, send, recv, device):
+        copy = remote(source, source, send, recv, device)
         copy.start()
-        p_copies.append(copy)
-    for step in range(1, 4):
-        spot = blocks.at[core, q, (p + 4 - step) % 4]
-        remote(spot, spot, p_send.at[step - 1], p_recv.at[step - 1], partner).wait_recv()
-        swap = remote(spot, spot, swap_send.at[step], swap_recv.at[step], partner)
-        swap.start()
-        swaps.append(swap)
-    q_copies = []
-    for step in range(1, 4):
-        copy = remote(
-            blocks.at[core, q], blocks.at[core, q], q_send.at[step - 1], q_recv.at[step - 1], at_pq(p, (q + step) % 4)
-        )
-        copy.start()
-        q_copies.append(copy)
-    for step in range(1, 4):
-        spot = blocks.at[core, (q + 4 - step) % 4]
-        remote(spot, spot, q_send.at[step - 1], q_recv.at[step - 1], partner).wait_recv()
-        swap = remote(spot, spot, swap_send.at[3 + step], swap_recv.at[3 + step], partner)
-        swap.start()
-        swaps.append(swap)
-    other = 1 - core
-    spot = blocks.at[other, p, q]
-    remote(spot, spot, swap_send.at[0], swap_recv.at[0], partner).wait_recv()
-    for step in range(1, 4):
-        spot = blocks.at[other, p, (q + 4 - step) % 4]
-        remote(spot, spot, swap_send.at[step], swap_recv.at[step], partner).wait_recv()
-    for step in range(1, 4):
-        spot = blocks.at[other, (p + 4 - step) % 4]
-        remote(spot, spot, swap_send.at[3 + step], swap_recv.at[3 + step], partner).wait_recv()
+        sent.append(copy)
+
+    def swap(dx, dy):
+        begin_copy(piece(core, dx, dy), swap_send.at[dx, dy], swap_recv.at[dx, dy], partner)
+
+    def third(a):
+        for step in (1, 3, 2):
+            dx, dy = offsets(a, 4 - step)
+            begin_copy(
+                piece(core, *offsets(a, 0)),
+                third_send.at[a, step - 1],
+                own_recv.at[dx, dy],
+                at_pq(p, (q + step) % 4),
+            )
+
+    def arrived(dx, dy):
+        spot = piece(core, dx, dy)
+        remote(spot, spot, swap_send.at[0, 0], own_recv.at[dx, dy], partner).wait_recv()
+        swap(dx, dy)
+
+    def swapped(dx, dy):
+        spot = piece(1 - core, dx, dy)
+        remote(spot, spot, swap_send.at[0, 0], swap_recv.at[dx, dy], partner).wait_recv()
+
+    for step in (1, 3, 2):
+        dx, dy = offsets(4 - step, 0)
+        begin_copy(
+            piece(core, 0, 0), second_send.at[step - 1], own_recv.at[dx, dy], at_pq((p + step) % 4, q)
+        )
+    third(0)
+    swap(0, 0)
+    for a in (3, 1):
+        arrived(*offsets(a, 0))
+        third(a)
+    for b in (3, 1):
+        arrived(*offsets(0, b))
+    arrived(*offsets(2, 0))
+    third(2)
+    arrived(*offsets(0, 2))
 
     left = lax.broadcasted_iota(jnp.int32, (24, LANES), 1) < 64
-
-    def unpack(index, carry):
-        x_at = index // 4
-        zl_at = index % 4
-        low_rows, high_rows = [], []
-        for y_at in range(4):
-            for zh_at in range(2):
-                if zh_at == 0:
-                    block = blocks[0, y_at, x_at, zl_at]
-                else:
-                    block = blocks[1, x_at, y_at, zl_at]
-                rounded = block.astype(BF16).astype(F32)
-                rest = block - rounded
-                low_rows.append(jnp.where(left, rounded, half_turn(rest)))
-                high_rows.append(jnp.where(left, half_turn(rounded), rest))
-        start = pl.multiple_of(index * 384, 128)
-        profile[pl.ds(start, BLOCK), :] = jnp.concatenate(low_rows, axis=0).astype(BF16)
-        profile[pl.ds(start + BLOCK, BLOCK), :] = jnp.concatenate(high_rows, axis=0).astype(BF16)
-        return carry
-
-    lax.fori_loop(0, 16, unpack, 0)
-    profile[LENGTH : LENGTH + WINDOW, :] = profile[0:WINDOW, :]
-
     begin = ((freq * 3 + 96 - 4) // 2) % ROWS
-    total[...] = jnp.zeros_like(total)
-
-    def filtered(tile, carry):
-        pieces = []
+    slab[0:128, :] = jnp.zeros((128, LANES), BF16)
+    slab[128 + SLAB : 256 + SLAB, :] = jnp.zeros((128, LANES), BF16)
+
+    def unpack(dx):
+        x_at = (x + dx) % 4
+
+        def unpack_one(zl_at, carry):
+            low_rows, high_rows = [], []
+            for y_at in range(4):
+                for colour in range(2):
+                    block = blocks[colour, x_at, y_at, zl_at]
+                    rounded = block.astype(BF16).astype(F32)
+                    rest = block - rounded
+                    low_rows.append(jnp.where(left, rounded, half_turn(rest)))
+                    high_rows.append(jnp.where(left, half_turn(rounded), rest))
+            rows = jnp.concatenate(low_rows + high_rows, axis=0).astype(BF16)
+            start = pl.multiple_of(zl_at * 384, 128)
+            slab[pl.ds(128 + start, 384), :] = rows
+            profile[pl.ds(pl.multiple_of(x_at * SLAB, 128) + start, 384), :] = rows
+            return carry
+
+        lax.fori_loop(0, 4, unpack_one, 0)
+
+    def filtered(dx):
+        first = ((x + dx) % 4) * 12 - 1 + 2 * ROWS - begin
+        lines = []
         for part in range(2):
             for row_block in (0, 2):
-                spot = 2 * tile + 2 * ROWS - begin - row_block
-                pieces.append(
-                    jnp.concatenate([toeplitz[part, spot % ROWS], toeplitz[part, (spot + 1) % ROWS]], axis=1)
+                lines.append(
+                    jnp.concatenate(
+                        [toeplitz[part, (first + step - row_block) % ROWS] for step in range(13)], axis=1
+                    )
                 )
-        start = pl.multiple_of(tile * 256, 128)
-        rows = jnp.concatenate([profile[pl.ds(start, 256), :], profile[pl.ds(start + 128, 256), :]], axis=1)
-        total[...] += jnp.dot(jnp.concatenate(pieces, axis=0), rows, preferred_element_type=F32)
-        return carry
-
-    lax.fori_loop(0, 24, filtered, 0)
+        rows = jnp.concatenate([slab[0 : 128 + SLAB, :], slab[128 : 256 + SLAB, :]], axis=1)
+        value = jnp.dot(jnp.concatenate(lines, axis=0), rows, preferred_element_type=F32)
+        if dx == 0:
+            total[...] = value
+        else:
+            total[...] += value
+
+    for dy in range(4):
+        swapped(0, dy)
+    unpack(0)
+    filtered(0)
+    for dy in (3, 1, 2):
+        arrived(3, dy)
+    for dy in (3, 1, 2):
+        arrived(1, dy)
+    for dy in range(4):
+        swapped(3, dy)
+    unpack(3)
+    filtered(3)
+    for dy in (3, 1, 2):
+        arrived(2, dy)
+    for dy in range(4):
+        swapped(1, dy)
+    unpack(1)
+    filtered(1)
+    for dy in range(4):
+        swapped(2, dy)
+    unpack(2)
+    filtered(2)
+
     for row_block in range(4):
         base = (row_block // 2) * 128
         cut = pl.ds((row_block % 2) * 128, 128)
         value = total[pl.ds(base, 128), cut] + total[pl.ds(256 + base, 128), cut]
         window[0, pl.ds(row_block * 128, 128), :] = value + half_turn(value)
-        start = pl.multiple_of(begin * 128 + row_block * 128, 128)
+        start = pl.multiple_of(((begin + row_block) % ROWS) * 128, 128)
         value = profile[pl.ds(start, 128), :].astype(F32)
         window[1, pl.ds(row_block * 128, 128), :] = value + half_turn(value)
 
@@ -452,7 +479,7 @@
         for copy in z_copies:
             copy.wait_send()
 
-    for copy in p_copies + q_copies + swaps:
+    for copy in sent:
         copy.wait_send()
 
     def drain(step, carry):
@@ -480,7 +507,8 @@
             pltpu.VMEM((24, LANES), F32),
             pltpu.VMEM((24, LANES), F32),
             pltpu.VMEM((2, 4, 4, 4, 24, LANES), F32),
-            pltpu.VMEM((LENGTH + WINDOW, LANES), BF16),
+            pltpu.VMEM((LENGTH, LANES), BF16),
+            pltpu.VMEM((SLAB + 256, LANES), BF16),
             pltpu.VMEM((3, 16, LANES), F32),
             pltpu.VMEM((LANES, LANES), F32),
             pltpu.VMEM((2, ROWS, LANES, LANES), BF16),
@@ -497,11 +525,10 @@
             dma((7,)),
             dma((4,)),
             dma((3,)),
-            dma((3,)),
-            dma((3,)),
-            dma((3,)),
-            dma((7,)),
-            dma((7,)),
+            dma((4, 3)),
+            dma((4, 4)),
+            dma((4, 4)),
+            dma((4, 4)),
             dma((14,)),
             dma((FREQ,)),
             dma((FREQ,)),

time: 52.8 us -> 45.8 us (0.87)
  Pallas kernels: 51.3 us -> 44.3 us
    pallas_call x1, Pallas kernels: 51.3 us -> 44.3 us  [on_device(): pl.pallas_call(kernel, out_shape=jax.ShapeDtypeStruct((OWN, COMP), F32),...]
where the time goes in v3:
time: 45.8 us; the launch traced here: 45.6 us
  Pallas kernels  44.3 us (97%)
  local copies, waits for them, and re-layouts  1.3 us (3%)
    pallas_call x1, Pallas kernels, on_device(): pl.pallas_call(kernel, out_shape=jax.ShapeDtypeStruct((OWN, COMP), F32),...  44.3 us
    unnamed x1, local copies, waits for them, and re-layouts  1.3 us

profile of v3, /device:TPU:1, one launch (start us, length us, event | category | flops | bytes accessed | tf_op | source)
XLA Modules:
  0.0 45.6 jit_solution(4272820087095678025)
XLA Ops:
  0.0 44.3 %shard_map.64 = f32[16,64]{1,0:T(8,128)} custom-call(f32[24,64]{1,0:T(8,128)} %elution_hbm.1, f32[8,64]{1,0:T(8,128)} %loadings_hbm.1, s32[8,64]{1,0:T(8,128)} %shifts_hbm.1, f32[48,128]{1,0:T(8,128)} %bitcast.3, f32[448,128]{1,0:T(8,128)} %constant.2.clone.tables_hbm, bf16[8,192,512]{2,1,0:T(8,128)(2,1)} %intensity_hbm.1), custom_call_target="tpu_custom_call" | custom-call | tf_op jit(solution)/shard_map/pallas_call | solution.py:495
  44.3 1.3 %copy.8 = f32[64,16]{0,1:T(8,128)} copy(f32[64,16]{0,1:T(8,128)} %bitcast.2) | data formatting | bytes 8192

commit v4 on v3

--- a/solution.py
+++ b/solution.py
@@ -24,6 +24,7 @@
 FREQ = 32
 OWN = 16
 SLAB = 1536
+STEPS = (1, 3, 2)
 WINDOW = 512
 
 
@@ -98,8 +99,8 @@
     weight_ref,
     tables_ref,
     samples,
-    mine,
-    theirs,
+    packed_rows,
+    gathered,
     blocks,
     profile,
     slab,
@@ -115,7 +116,6 @@
     num_send,
     num_recv,
     load_sems,
-    pair_sem,
     z_send,
     z_recv,
     second_send,
@@ -134,14 +134,8 @@
     x = freq // 8
     y = mz // 2
     z_hi = mz % 2
-    p = x * (1 - core) + y * core
-    q = y * (1 - core) + x * core
-
     def at(x_to, y_to, z_to, core_to):
         return (x_to * 8 + (z_to % 4) * 2 + core_to, y_to * 2 + z_to // 4)
-
-    def at_pq(p_to, q_to):
-        return at(p_to * (1 - core) + q_to * core, q_to * (1 - core) + p_to * core, z_hi * 4 + z_lo, core)
 
     partner = (freq + 1 - 2 * core, mz)
     z_mine = z_hi * 4 + z_lo
@@ -172,14 +166,18 @@
         pl.semaphore_signal(
             barrier, inc=1, device_id=(freq, ((y + step) % 4) * 2 + z_hi), device_id_type=MESH
         )
-    for step in range(4):
+    for step in range(8):
         pl.semaphore_signal(
-            barrier, inc=1, device_id=at(x, y, (1 - z_hi) * 4 + step, core), device_id_type=MESH
+            barrier,
+            inc=1,
+            device_id=at(x, y, (1 - z_hi) * 4 + step % 4, step // 4),
+            device_id_type=MESH,
         )
 
     loads[0].wait()
     own_rows = elution_ref[...]
-    mine[...] = jnp.concatenate([own_rows, own_rows], axis=1)
+    beside = jnp.concatenate([own_rows[16:24], own_rows[16:24]], axis=0)
+    packed_rows[...] = jnp.concatenate([own_rows[0:16], beside], axis=1)
 
     loads[1].wait()
     loads[2].wait()
@@ -189,29 +187,126 @@
     for z in range(3):
         lags[z] = lag_rows[z]
 
-    pl.semaphore_wait(barrier, FREQ - 1 + 3 + 4)
+    pl.semaphore_wait(barrier, FREQ - 1 + 3 + 8)
 
     def remote(source, target, send, recv, device):
         return pltpu.make_async_remote_copy(
             src_ref=source, dst_ref=target, send_sem=send, recv_sem=recv, device_id=device, device_id_type=MESH
         )
 
-    pair = remote(mine, theirs, pair_sem.at[0], pair_sem.at[1], partner)
-    pair.start()
-    pair.wait()
-    lane24 = lax.broadcasted_iota(jnp.int32, (24, LANES), 1)
-    side = (lane24 // 64) == core
-    z_copies = []
-    for step in range(1, 8):
-        own = blocks.at[core, x, y, z_lo]
-        z_to = (z_mine + step) % 8
-        z_copies.append(remote(own, own, z_send.at[step - 1], z_recv.at[z_lo], at(x, y, z_to, core)))
+    z_copies = [
+        remote(
+            packed_rows,
+            gathered.at[z_lo, core],
+            z_send.at[step],
+            z_recv.at[z_lo, core],
+            at(x, y, (z_mine + step) % 8, z_hi),
+        )
+        for step in range(8)
+    ]
+    for copy in z_copies[1:]:
+        copy.start()
+
+    @pl.when(z_hi != core)
+    def _():
+        z_copies[0].start()
 
     @pl.when(z_hi == core)
     def _():
-        blocks[core, x, y, z_lo] = jnp.where(side, mine[...], theirs[...])
-        for copy in z_copies:
-            copy.start()
+        gathered[z_lo, core] = packed_rows[...]
+
+    close = z_lo // 2
+    near = close * (1 - abs(z_hi - core)) + (1 - close) * abs(z_hi - core)
+
+    def half_of(colour_is_own, half):
+        return near if (half == 0) == colour_is_own else 1 - near
+
+    left16 = lax.broadcasted_iota(jnp.int32, (16, LANES), 1) < 64
+    left8 = left16[:8]
+
+    def merge(half):
+        for index in range(2):
+            source = 2 * half_of(True, half) + index
+            for source_core in range(2):
+                itself = jnp.logical_and(z_hi == core, jnp.logical_and(z_lo == source, core == source_core))
+
+                @pl.when(jnp.logical_not(itself))
+                def _(source=source, source_core=source_core):
+                    spot = gathered.at[source, source_core]
+                    remote(packed_rows, spot, z_send.at[0], z_recv.at[source, source_core], partner).wait_recv()
+
+            zero, one = gathered[source, 0], gathered[source, 1]
+            blocks[core, x, y, source, 0:16] = jnp.where(left16, zero, half_turn(one))
+            blocks[core, x, y, source, 16:24] = jnp.where(left8, half_turn(zero[:8]), one[:8])
+
+    def piece(colour_is_own, colour, dx, dy, half):
+        start = 2 * half_of(colour_is_own, half)
+        return blocks.at[colour, (x + dx) % 4, (y + dy) % 4, pl.ds(start, 2)]
+
+    class Colour:
+        def __init__(self, colour):
+            self.colour = colour
+
+        def offsets(self, a, b):
+            return (a, b) if self.colour == 0 else (b, a)
+
+        def send(self, a, b, a_step, b_step, half, sem):
+            source = piece(True, self.colour, *self.offsets(a, b), half)
+            to_x, to_y = self.offsets(a_step, b_step)
+            dx, dy = self.offsets((a - a_step) % 4, (b - b_step) % 4)
+            device = at((x + to_x) % 4, (y + to_y) % 4, z_mine, self.colour)
+            remote(source, source, sem, own_recv.at[dx, dy, half], device).start()
+
+        def second(self, half):
+            for step in STEPS:
+                self.send(0, 0, step, 0, half, second_send.at[step - 1, half])
+
+        def third(self, a, half):
+            for step in STEPS:
+                self.send(a, 0, 0, step, half, third_send.at[a, step - 1, half])
+
+        def arrived(self, a, b, half):
+            dx, dy = self.offsets(a, b)
+            spot = piece(True, self.colour, dx, dy, half)
+            remote(spot, spot, swap_send.at[0, 0, 0], own_recv.at[dx, dy, half], partner).wait_recv()
+            if b == 0:
+                self.third(a, half)
+            self.swap(dx, dy, half)
+
+        def swap(self, dx, dy, half):
+            spot = piece(True, self.colour, dx, dy, half)
+            remote(spot, spot, swap_send.at[dx, dy, half], swap_recv.at[dx, dy, half], partner).start()
+
+        def open_up(self, half):
+            if self.colour == 0:
+                self.third(0, half)
+                self.second(half)
+            else:
+                self.second(half)
+                self.third(0, half)
+            self.swap(0, 0, half)
+
+        def first_arrivals(self, half):
+            for a, b in ((3, 0), (1, 0), (0, 3), (0, 1), (2, 0), (0, 2)):
+                self.arrived(a, b, half)
+
+    def for_each_core(action):
+        for colour in range(2):
+            pl.when(core == colour)(functools.partial(action, Colour(colour)))
+
+    def swapped(dx):
+        for half in range(2):
+            for dy in range(4):
+                spot = piece(False, 1 - core, dx, dy, half)
+                remote(spot, spot, swap_send.at[0, 0, 0], swap_recv.at[dx, dy, half], partner).wait_recv()
+
+    def arrivals(spots):
+        def action(colour):
+            for half in range(2):
+                for dx, dy in spots:
+                    colour.arrived(*colour.offsets(dx, dy), half)
+
+        return action
 
     row = lax.broadcasted_iota(jnp.int32, (LANES, LANES), 0)
     lane = lax.broadcasted_iota(jnp.int32, (LANES, LANES), 1)
@@ -232,68 +327,17 @@
 
     lax.fori_loop(0, 16, build, turned(2, 15))
 
-    for source in range(4):
-
-        @pl.when(jnp.logical_or(z_hi != core, z_lo != source))
-        def _(source=source):
-            spot = blocks.at[core, x, y, source]
-            remote(spot, spot, z_send.at[0], z_recv.at[source], partner).wait_recv()
-
-    def offsets(a, b):
-        return (a * (1 - core) + b * core, b * (1 - core) + a * core)
-
-    def piece(colour, dx, dy):
-        return blocks.at[colour, (x + dx) % 4, (y + dy) % 4]
-
-    sent = []
-
-    def begin_copy(source, send, recv, device):
-        copy = remote(source, source, send, recv, device)
-        copy.start()
-        sent.append(copy)
-
-    def swap(dx, dy):
-        begin_copy(piece(core, dx, dy), swap_send.at[dx, dy], swap_recv.at[dx, dy], partner)
-
-    def third(a):
-        for step in (1, 3, 2):
-            dx, dy = offsets(a, 4 - step)
-            begin_copy(
-                piece(core, *offsets(a, 0)),
-                third_send.at[a, step - 1],
-                own_recv.at[dx, dy],
-                at_pq(p, (q + step) % 4),
-            )
-
-    def arrived(dx, dy):
-        spot = piece(core, dx, dy)
-        remote(spot, spot, swap_send.at[0, 0], own_recv.at[dx, dy], partner).wait_recv()
-        swap(dx, dy)
-
-    def swapped(dx, dy):
-        spot = piece(1 - core, dx, dy)
-        remote(spot, spot, swap_send.at[0, 0], swap_recv.at[dx, dy], partner).wait_recv()
-
-    for step in (1, 3, 2):
-        dx, dy = offsets(4 - step, 0)
-        begin_copy(
-            piece(core, 0, 0), second_send.at[step - 1], own_recv.at[dx, dy], at_pq((p + step) % 4, q)
-        )
-    third(0)
-    swap(0, 0)
-    for a in (3, 1):
-        arrived(*offsets(a, 0))
-        third(a)
-    for b in (3, 1):
-        arrived(*offsets(0, b))
-    arrived(*offsets(2, 0))
-    third(2)
-    arrived(*offsets(0, 2))
+    merge(0)
+    for_each_core(lambda colour: colour.open_up(0))
+    merge(1)
+    for_each_core(lambda colour: colour.open_up(1))
+    slab[0:128, :] = jnp.zeros((128, LANES), BF16)
+    slab[128 + SLAB : 256 + SLAB, :] = jnp.zeros((128, LANES), BF16)
+    for_each_core(lambda colour: colour.first_arrivals(0))
+    for_each_core(lambda colour: colour.first_arrivals(1))
 
     left = lax.broadcasted_iota(jnp.int32, (24, LANES), 1) < 64
     begin = ((freq * 3 + 96 - 4) // 2) % ROWS
-    slab[0:128, :] = jnp.zeros((128, LANES), BF16)
-    slab[128 + SLAB : 256 + SLAB, :] = jnp.zeros((128, LANES), BF16)
 
     def unpack(dx):
         x_at = (x + dx) % 4
@@ -332,26 +376,18 @@
         else:
             total[...] += value
 
-    for dy in range(4):
-        swapped(0, dy)
+    swapped(0)
     unpack(0)
     filtered(0)
-    for dy in (3, 1, 2):
-        arrived(3, dy)
-    for dy in (3, 1, 2):
-        arrived(1, dy)
-    for dy in range(4):
-        swapped(3, dy)
+    for_each_core(arrivals(((3, 3), (3, 1), (3, 2), (1, 3), (1, 1), (1, 2))))
+    swapped(3)
     unpack(3)
     filtered(3)
-    for dy in (3, 1, 2):
-        arrived(2, dy)
-    for dy in range(4):
-        swapped(1, dy)
+    for_each_core(arrivals(((2, 3), (2, 1), (2, 2))))
+    swapped(1)
     unpack(1)
     filtered(1)
-    for dy in range(4):
-        swapped(2, dy)
+    swapped(2)
     unpack(2)
     filtered(2)
 
@@ -474,13 +510,22 @@
         own_channels, inverse, (((1,), (1,)), ((), ())), precision=HIGHEST, preferred_element_type=F32
     )
 
-    @pl.when(z_hi == core)
+    for copy in z_copies[1:]:
+        copy.wait_send()
+
+    @pl.when(z_hi != core)
     def _():
-        for copy in z_copies:
-            copy.wait_send()
-
-    for copy in sent:
-        copy.wait_send()
+        z_copies[0].wait_send()
+
+    part = blocks.at[0, 0, 0, 0:2]
+    for half in range(2):
+        for step in range(3):
+            remote(part, part, second_send.at[step, half], z_recv.at[0, 0], partner).wait_send()
+            for a in range(4):
+                remote(part, part, third_send.at[a, step, half], z_recv.at[0, 0], partner).wait_send()
+        for dx in range(4):
+            for dy in range(4):
+                remote(part, part, swap_send.at[dx, dy, half], z_recv.at[0, 0], partner).wait_send()
 
     def drain(step, carry):
         num_copy(step).wait_send()
@@ -492,6 +537,9 @@
 def on_device(intensity, elution, loadings, shifts, bin_weight):
     vmem = pl.BlockSpec(memory_space=pltpu.VMEM)
     dma = pltpu.SemaphoreType.DMA
+    def held(value):
+        return pltpu.with_memory_space_constraint(value, pltpu.HBM)
+
     by_channel = pl.pallas_call(
         kernel,
         out_shape=jax.ShapeDtypeStruct((OWN, COMP), F32),
@@ -504,8 +552,8 @@
             pltpu.VMEM((ROWS, LANES), F32),
             pltpu.VMEM((448, LANES), F32),
             pltpu.VMEM((RUNS, BLOCK, CHANNELS), BF16),
-            pltpu.VMEM((24, LANES), F32),
-            pltpu.VMEM((24, LANES), F32),
+            pltpu.VMEM((16, LANES), F32),
+            pltpu.VMEM((4, 2, 16, LANES), F32),
             pltpu.VMEM((2, 4, 4, 4, 24, LANES), F32),
             pltpu.VMEM((LENGTH, LANES), BF16),
             pltpu.VMEM((SLAB + 256, LANES), BF16),
@@ -521,22 +569,21 @@
             pltpu.VMEM((FREQ, 8, LANES), F32),
             pltpu.VMEM((FREQ, 8, LANES), F32),
             dma((6,)),
-            dma((2,)),
-            dma((7,)),
-            dma((4,)),
-            dma((3,)),
-            dma((4, 3)),
-            dma((4, 4)),
-            dma((4, 4)),
-            dma((4, 4)),
+            dma((8,)),
+            dma((4, 2)),
+            dma((3, 2)),
+            dma((4, 3, 2)),
+            dma((4, 4, 2)),
+            dma((4, 4, 2)),
+            dma((4, 4, 2)),
             dma((14,)),
             dma((FREQ,)),
             dma((FREQ,)),
         ],
         compiler_params=pltpu.CompilerParams(
-            collective_id=0, has_side_effects=True, vmem_limit_bytes=67043328
+            collective_id=0, has_side_effects=True, vmem_limit_bytes=32 * 1024 * 1024
         ),
-    )(elution, loadings, shifts, bin_weight.reshape(ROWS, LANES), transform_tables(), intensity)
+    )(*map(held, (elution, loadings, shifts, bin_weight.reshape(ROWS, LANES), transform_tables(), intensity)))
     return by_channel.T
 
 

time: 45.8 us -> 44.6 us (0.974)
  local copies, waits for them, and re-layouts: 1.3 us -> 0.6 us
  Pallas kernels: 44.3 us -> 43.8 us
    unnamed x1, local copies, waits for them, and re-layouts: 1.3 us -> 0.6 us
where the time goes in v4:
time: 44.6 us; the launch traced here: 44.4 us
  Pallas kernels  43.8 us (98%)
  local copies, waits for them, and re-layouts  0.6 us (1%)
    pallas_call x1, Pallas kernels, on_device(): pl.pallas_call(kernel, out_shape=jax.ShapeDtypeStruct((OWN, COMP), F32),...  43.8 us

profile of v4, /device:TPU:1, one launch (start us, length us, event | category | flops | bytes accessed | tf_op | source)
XLA Modules:
  0.0 44.4 jit_solution(2273486559817814126)
XLA Ops:
  0.0 43.8 %shard_map.64 = f32[16,64]{1,0:T(8,128)S(1)} custom-call(f32[24,64]{1,0:T(8,128)} %elution_hbm.1, f32[8,64]{1,0:T(8,128)} %loadings_hbm.1, s32[8,64]{1,0:T(8,128)} %shifts_hbm.1, f32[48,128]{1,0:T(8,128)} %bitcast.3, f32[448,128]{1,0:T(8,128)} %constant.2.clone.tables_hbm, bf16[8,192,512]{2,1,0:T(8,128)(2,1)} %intensity_hbm.1), custom_call_target="tpu_custom_call" | custom-call | tf_op jit(solution)/shard_map/pallas_call | solution.py:543
  43.8 0.6 %copy.8 = f32[64,16]{0,1:T(8,128)} copy(f32[64,16]{0,1:T(8,128)S(1)} %bitcast.2) | data formatting | bytes 8192

commit v5 on v4

--- a/solution.py
+++ b/solution.py
@@ -124,8 +124,7 @@
     swap_send,
     swap_recv,
     gram_sems,
-    num_sems,
-    num_recv_sems,
+    num_sem,
 ):
     freq = lax.axis_index("freq")
     mz = lax.axis_index("mz")
@@ -140,6 +139,24 @@
     partner = (freq + 1 - 2 * core, mz)
     z_mine = z_hi * 4 + z_lo
 
+    barrier = pltpu.get_barrier_semaphore()
+
+    for step in range(8):
+        pl.semaphore_signal(
+            barrier,
+            inc=1,
+            device_id=at(x, y, (1 - z_hi) * 4 + step % 4, step // 4),
+            device_id_type=MESH,
+        )
+    for step in range(1, 4):
+        pl.semaphore_signal(
+            barrier, inc=1, device_id=(freq, ((y + step) % 4) * 2 + z_hi), device_id_type=MESH
+        )
+    def greet(step, carry):
+        pl.semaphore_signal(barrier, inc=1, device_id=((freq + step) % FREQ, mz), device_id_type=MESH)
+        return carry
+
+    lax.fori_loop(1, FREQ, greet, 0)
     loads = [
         pltpu.make_async_copy(source, target, load_sems.at[index])
         for index, (source, target) in enumerate(
@@ -155,25 +172,6 @@
     ]
     for load in loads:
         load.start()
-    barrier = pltpu.get_barrier_semaphore()
-
-    def greet(step, carry):
-        pl.semaphore_signal(barrier, inc=1, device_id=((freq + step) % FREQ, mz), device_id_type=MESH)
-        return carry
-
-    lax.fori_loop(1, FREQ, greet, 0)
-    for step in range(1, 4):
-        pl.semaphore_signal(
-            barrier, inc=1, device_id=(freq, ((y + step) % 4) * 2 + z_hi), device_id_type=MESH
-        )
-    for step in range(8):
-        pl.semaphore_signal(
-            barrier,
-            inc=1,
-            device_id=at(x, y, (1 - z_hi) * 4 + step % 4, step // 4),
-            device_id_type=MESH,
-        )
-
     loads[0].wait()
     own_rows = elution_ref[...]
     beside = jnp.concatenate([own_rows[16:24], own_rows[16:24]], axis=0)
@@ -259,23 +257,23 @@
 
         def second(self, half):
             for step in STEPS:
-                self.send(0, 0, step, 0, half, second_send.at[step - 1, half])
+                self.send(0, 0, step, 0, half, second_send)
 
         def third(self, a, half):
             for step in STEPS:
-                self.send(a, 0, 0, step, half, third_send.at[a, step - 1, half])
+                self.send(a, 0, 0, step, half, third_send)
 
         def arrived(self, a, b, half):
             dx, dy = self.offsets(a, b)
             spot = piece(True, self.colour, dx, dy, half)
-            remote(spot, spot, swap_send.at[0, 0, 0], own_recv.at[dx, dy, half], partner).wait_recv()
+            remote(spot, spot, swap_send, own_recv.at[dx, dy, half], partner).wait_recv()
             if b == 0:
                 self.third(a, half)
             self.swap(dx, dy, half)
 
         def swap(self, dx, dy, half):
             spot = piece(True, self.colour, dx, dy, half)
-            remote(spot, spot, swap_send.at[dx, dy, half], swap_recv.at[dx, dy, half], partner).start()
+            remote(spot, spot, swap_send, swap_recv.at[dx, dy, half], partner).start()
 
         def open_up(self, half):
             if self.colour == 0:
@@ -298,7 +296,7 @@
         for half in range(2):
             for dy in range(4):
                 spot = piece(False, 1 - core, dx, dy, half)
-                remote(spot, spot, swap_send.at[0, 0, 0], swap_recv.at[dx, dy, half], partner).wait_recv()
+                remote(spot, spot, swap_send, swap_recv.at[dx, dy, half], partner).wait_recv()
 
     def arrivals(spots):
         def action(colour):
@@ -371,25 +369,27 @@
                 )
         rows = jnp.concatenate([slab[0 : 128 + SLAB, :], slab[128 : 256 + SLAB, :]], axis=1)
         value = jnp.dot(jnp.concatenate(lines, axis=0), rows, preferred_element_type=F32)
-        if dx == 0:
-            total[...] = value
-        else:
-            total[...] += value
-
-    swapped(0)
-    unpack(0)
-    filtered(0)
-    for_each_core(arrivals(((3, 3), (3, 1), (3, 2), (1, 3), (1, 1), (1, 2))))
-    swapped(3)
-    unpack(3)
-    filtered(3)
-    for_each_core(arrivals(((2, 3), (2, 1), (2, 2))))
-    swapped(1)
-    unpack(1)
-    filtered(1)
-    swapped(2)
-    unpack(2)
-    filtered(2)
+        total[...] += value
+
+    total[...] = jnp.zeros_like(total)
+
+    def slab_step(index, carry):
+        dx = jnp.where(index == 0, 0, jnp.where(index == 1, 3, index - 1))
+        swapped(dx)
+        unpack(dx)
+        filtered(dx)
+
+        @pl.when(index == 0)
+        def _():
+            for_each_core(arrivals(((3, 3), (3, 1), (3, 2), (1, 3), (1, 1), (1, 2))))
+
+        @pl.when(index == 1)
+        def _():
+            for_each_core(arrivals(((2, 3), (2, 1), (2, 2))))
+
+        return carry
+
+    lax.fori_loop(0, 4, slab_step, 0)
 
     for row_block in range(4):
         base = (row_block // 2) * 128
@@ -441,7 +441,7 @@
 
     def num_copy(step):
         to = (freq + step) % FREQ
-        return remote(num_send.at[to], num_recv.at[freq], num_sems.at[step], num_recv_sems.at[step], (to, mz))
+        return remote(num_send.at[to], num_recv.at[freq], num_sem.at[0], num_sem.at[1], (to, mz))
 
     def send_num(step, carry):
         num_copy(step).start()
@@ -460,6 +460,16 @@
         )
         copy.start()
         x_copies.append(copy)
+    for copy in z_copies[1:]:
+        copy.wait_send()
+
+    @pl.when(z_hi != core)
+    def _():
+        z_copies[0].wait_send()
+
+    for spot, sem in ((blocks.at[0, 0, 0:3], second_send), (blocks.at[0, 0:3], third_send), (blocks.at[0], swap_send)):
+        remote(spot, spot, sem, z_recv.at[0, 0], partner).wait_send()
+
     for copy in x_copies:
         copy.wait()
     gram_send[2] = (gram_send[1] + gram_x[0]) + (gram_x[1] + gram_x[2])
@@ -496,13 +506,9 @@
         matrix = jnp.where(row64 == step, top_new, jnp.where(row64 == step + 1, low_new, rest))
     inverse = matrix[:, COMP:]
 
-    def wait_num(step, carry):
-        source = (freq + FREQ - step) % FREQ
-        copy = remote(num_send.at[source], num_recv.at[source], num_sems.at[step], num_recv_sems.at[step], (source, mz))
-        copy.wait_recv()
-        return carry
-
-    lax.fori_loop(1, FREQ, wait_num, 0)
+    others = num_send.at[0 : FREQ - 1]
+    num_all = remote(others, num_recv.at[0 : FREQ - 1], num_sem.at[0], num_sem.at[1], partner)
+    num_all.wait_recv()
     num_recv[freq] = num_send[freq]
     summed = jnp.sum(num_recv[...], axis=0)
     own_channels = jnp.concatenate([summed[:, :64], summed[:, 64:]], axis=0)
@@ -510,28 +516,7 @@
         own_channels, inverse, (((1,), (1,)), ((), ())), precision=HIGHEST, preferred_element_type=F32
     )
 
-    for copy in z_copies[1:]:
-        copy.wait_send()
-
-    @pl.when(z_hi != core)
-    def _():
-        z_copies[0].wait_send()
-
-    part = blocks.at[0, 0, 0, 0:2]
-    for half in range(2):
-        for step in range(3):
-            remote(part, part, second_send.at[step, half], z_recv.at[0, 0], partner).wait_send()
-            for a in range(4):
-                remote(part, part, third_send.at[a, step, half], z_recv.at[0, 0], partner).wait_send()
-        for dx in range(4):
-            for dy in range(4):
-                remote(part, part, swap_send.at[dx, dy, half], z_recv.at[0, 0], partner).wait_send()
-
-    def drain(step, carry):
-        num_copy(step).wait_send()
-        return carry
-
-    lax.fori_loop(1, FREQ, drain, 0)
+    num_all.wait_send()
 
 
 def on_device(intensity, elution, loadings, shifts, bin_weight):
@@ -571,14 +556,13 @@
             dma((6,)),
             dma((8,)),
             dma((4, 2)),
-            dma((3, 2)),
-            dma((4, 3, 2)),
+            dma,
+            dma,
             dma((4, 4, 2)),
-            dma((4, 4, 2)),
+            dma,
             dma((4, 4, 2)),
             dma((14,)),
-            dma((FREQ,)),
-            dma((FREQ,)),
+            dma((2,)),
         ],
         compiler_params=pltpu.CompilerParams(
             collective_id=0, has_side_effects=True, vmem_limit_bytes=32 * 1024 * 1024

time: 44.6 us -> 42 us (0.942)
  Pallas kernels: 43.8 us -> 41.3 us
    pallas_call x1, Pallas kernels: 43.8 us -> 41.3 us  [on_device(): pl.pallas_call(kernel, out_shape=jax.ShapeDtypeStruct((OWN, COMP), F32),...]
where the time goes in v5:
time: 42 us; the launch traced here: 41.9 us
  Pallas kernels  41.3 us (98%)
  local copies, waits for them, and re-layouts  0.6 us (1%)
    pallas_call x1, Pallas kernels, on_device(): pl.pallas_call(kernel, out_shape=jax.ShapeDtypeStruct((OWN, COMP), F32),...  41.3 us

profile of v5, /device:TPU:1, one launch (start us, length us, event | category | flops | bytes accessed | tf_op | source)
XLA Modules:
  0.0 41.9 jit_solution(16206563129739793938)
XLA Ops:
  0.0 41.3 %shard_map.64 = f32[16,64]{1,0:T(8,128)S(1)} custom-call(f32[24,64]{1,0:T(8,128)} %elution_hbm.1, f32[8,64]{1,0:T(8,128)} %loadings_hbm.1, s32[8,64]{1,0:T(8,128)} %shifts_hbm.1, f32[48,128]{1,0:T(8,128)} %bitcast.3, f32[448,128]{1,0:T(8,128)} %constant.2.clone.tables_hbm, bf16[8,192,512]{2,1,0:T(8,128)(2,1)} %intensity_hbm.1), custom_call_target="tpu_custom_call" | custom-call | tf_op jit(solution)/shard_map/pallas_call | solution.py:528
  41.3 0.6 %copy.8 = f32[64,16]{0,1:T(8,128)} copy(f32[64,16]{0,1:T(8,128)S(1)} %bitcast.2) | data formatting | bytes 8192

commit v6 on v5

--- a/solution.py
+++ b/solution.py
@@ -114,6 +114,8 @@
     gram_x,
     gram_z,
     num_send,
+    num_core,
+    num_half,
     num_recv,
     load_sems,
     z_send,
@@ -139,24 +141,6 @@
     partner = (freq + 1 - 2 * core, mz)
     z_mine = z_hi * 4 + z_lo
 
-    barrier = pltpu.get_barrier_semaphore()
-
-    for step in range(8):
-        pl.semaphore_signal(
-            barrier,
-            inc=1,
-            device_id=at(x, y, (1 - z_hi) * 4 + step % 4, step // 4),
-            device_id_type=MESH,
-        )
-    for step in range(1, 4):
-        pl.semaphore_signal(
-            barrier, inc=1, device_id=(freq, ((y + step) % 4) * 2 + z_hi), device_id_type=MESH
-        )
-    def greet(step, carry):
-        pl.semaphore_signal(barrier, inc=1, device_id=((freq + step) % FREQ, mz), device_id_type=MESH)
-        return carry
-
-    lax.fori_loop(1, FREQ, greet, 0)
     loads = [
         pltpu.make_async_copy(source, target, load_sems.at[index])
         for index, (source, target) in enumerate(
@@ -172,18 +156,28 @@
     ]
     for load in loads:
         load.start()
+    barrier = pltpu.get_barrier_semaphore()
+
+    for step in range(8):
+        pl.semaphore_signal(
+            barrier,
+            inc=1,
+            device_id=at(x, y, (1 - z_hi) * 4 + step % 4, step // 4),
+            device_id_type=MESH,
+        )
+    for step in range(1, 4):
+        pl.semaphore_signal(
+            barrier, inc=1, device_id=(freq, ((y + step) % 4) * 2 + z_hi), device_id_type=MESH
+        )
+    def greet(step, carry):
+        pl.semaphore_signal(barrier, inc=1, device_id=((freq + step) % FREQ, mz), device_id_type=MESH)
+        return carry
+
+    lax.fori_loop(1, FREQ, greet, 0)
     loads[0].wait()
     own_rows = elution_ref[...]
     beside = jnp.concatenate([own_rows[16:24], own_rows[16:24]], axis=0)
     packed_rows[...] = jnp.concatenate([own_rows[0:16], beside], axis=1)
-
-    loads[1].wait()
-    loads[2].wait()
-    lag_rows = lag_weights(
-        weight_ref[...], tables_ref[:96, :ROWS], tables_ref[96:192], tables_ref[192:448], flip
-    )
-    for z in range(3):
-        lags[z] = lag_rows[z]
 
     pl.semaphore_wait(barrier, FREQ - 1 + 3 + 8)
 
@@ -305,6 +299,14 @@
                     colour.arrived(*colour.offsets(dx, dy), half)
 
         return action
+
+    loads[1].wait()
+    loads[2].wait()
+    lag_rows = lag_weights(
+        weight_ref[...], tables_ref[:96, :ROWS], tables_ref[96:192], tables_ref[192:448], flip
+    )
+    for z in range(3):
+        lags[z] = lag_rows[z]
 
     row = lax.broadcasted_iota(jnp.int32, (LANES, LANES), 0)
     lane = lax.broadcasted_iota(jnp.int32, (LANES, LANES), 1)
@@ -436,15 +438,16 @@
             jnp.concatenate([high[cut], low[cut]], axis=0), samples[run], preferred_element_type=F32
         )
         numer = numer + both[:64] + both[64:]
-    by_channel = jnp.transpose(numer).reshape(FREQ, 2, 8, COMP)
-    num_send[...] = jnp.concatenate([by_channel[:, 0], by_channel[:, 1]], axis=2)
-
-    def num_copy(step):
-        to = (freq + step) % FREQ
-        return remote(num_send.at[to], num_recv.at[freq], num_sem.at[0], num_sem.at[1], (to, mz))
+    by_channel = jnp.transpose(numer).reshape(FREQ // 2, 2, 2, 8, COMP)
+    for side in range(2):
+        num_send[side] = jnp.concatenate([by_channel[:, side, 0], by_channel[:, side, 1]], axis=2)
+    num_swap = remote(num_send.at[1 - core], num_core, num_sem.at[2], num_sem.at[3], partner)
+    num_swap.start()
+    chip = freq // 2
 
     def send_num(step, carry):
-        num_copy(step).start()
+        to = (chip + step) % (FREQ // 2)
+        remote(num_half.at[to], num_recv.at[chip], num_sem.at[0], num_sem.at[1], (2 * to + core, mz)).start()
         return carry
 
     core_copy.wait()
@@ -484,7 +487,9 @@
         )
         copy.start()
         z_grams.append(copy)
-    lax.fori_loop(1, FREQ, send_num, 0)
+    num_swap.wait()
+    num_half[...] = num_send[core] + num_core[...]
+    lax.fori_loop(1, FREQ // 2, send_num, 0)
     for copy in z_grams:
         copy.wait()
     packed = (gram_send[2] + gram_z[0]) + (gram_z[1] + gram_z[2])
@@ -493,23 +498,30 @@
     lane64 = lax.broadcasted_iota(jnp.int32, (COMP, LANES), 1)
     unit = (lane64 == row64 + COMP).astype(F32)
     matrix = jnp.where(lane64 < COMP, jnp.concatenate([packed, half_turn(packed)], axis=0), unit)
-    for step in range(0, COMP, 2):
-        one = jnp.broadcast_to(matrix[:, step : step + 1], matrix.shape)
-        two = jnp.broadcast_to(matrix[:, step + 1 : step + 2], matrix.shape)
-        top, low = matrix[step : step + 1], matrix[step + 1 : step + 2]
+    def clear(value, top, low, columns, step):
+        one, two = columns
         one_top, one_low = one[step : step + 1], one[step + 1 : step + 2]
         two_top, two_low = two[step : step + 1], two[step + 1 : step + 2]
         scale = 1.0 / (one_top * two_low - two_top * one_low)
         top_new = (two_low * top - two_top * low) * scale
         low_new = (one_top * low - one_low * top) * scale
-        rest = matrix - one * top_new - two * low_new
-        matrix = jnp.where(row64 == step, top_new, jnp.where(row64 == step + 1, low_new, rest))
+        rest = value - one * top_new - two * low_new
+        return jnp.where(row64 == step, top_new, jnp.where(row64 == step + 1, low_new, rest))
+
+    for step in range(0, COMP, 4):
+        columns = [jnp.broadcast_to(matrix[:, at_ : at_ + 1], matrix.shape) for at_ in range(step, step + 4)]
+        first_two = columns[:2]
+        last_two = [
+            clear(value, value[step : step + 1], value[step + 1 : step + 2], first_two, step) for value in columns[2:]
+        ]
+        matrix = clear(matrix, matrix[step : step + 1], matrix[step + 1 : step + 2], first_two, step)
+        matrix = clear(matrix, matrix[step + 2 : step + 3], matrix[step + 3 : step + 4], last_two, step + 2)
     inverse = matrix[:, COMP:]
 
-    others = num_send.at[0 : FREQ - 1]
-    num_all = remote(others, num_recv.at[0 : FREQ - 1], num_sem.at[0], num_sem.at[1], partner)
+    others = num_recv.at[0 : FREQ // 2 - 1]
+    num_all = remote(others, others, num_sem.at[0], num_sem.at[1], partner)
     num_all.wait_recv()
-    num_recv[freq] = num_send[freq]
+    num_recv[chip] = num_half[chip]
     summed = jnp.sum(num_recv[...], axis=0)
     own_channels = jnp.concatenate([summed[:, :64], summed[:, 64:]], axis=0)
     out_ref[...] = lax.dot_general(
@@ -551,8 +563,10 @@
             pltpu.VMEM((32, LANES), F32),
             pltpu.VMEM((3, 32, LANES), F32),
             pltpu.VMEM((3, 32, LANES), F32),
-            pltpu.VMEM((FREQ, 8, LANES), F32),
-            pltpu.VMEM((FREQ, 8, LANES), F32),
+            pltpu.VMEM((2, FREQ // 2, 8, LANES), F32),
+            pltpu.VMEM((FREQ // 2, 8, LANES), F32),
+            pltpu.VMEM((FREQ // 2, 8, LANES), F32),
+            pltpu.VMEM((FREQ // 2, 8, LANES), F32),
             dma((6,)),
             dma((8,)),
             dma((4, 2)),
@@ -562,7 +576,7 @@
             dma,
             dma((4, 4, 2)),
             dma((14,)),
-            dma((2,)),
+            dma((4,)),
         ],
         compiler_params=pltpu.CompilerParams(
             collective_id=0, has_side_effects=True, vmem_limit_bytes=32 * 1024 * 1024

time: 42 us -> 39 us (0.929)
  Pallas kernels: 41.3 us -> 38.3 us
    pallas_call x1, Pallas kernels: 41.3 us -> 38.3 us  [on_device(): pl.pallas_call(kernel, out_shape=jax.ShapeDtypeStruct((OWN, COMP), F32),...]
where the time goes in v6:
time: 39 us; the launch traced here: 38.9 us
  Pallas kernels  38.3 us (98%)
  local copies, waits for them, and re-layouts  0.6 us (2%)
    pallas_call x1, Pallas kernels, on_device(): pl.pallas_call(kernel, out_shape=jax.ShapeDtypeStruct((OWN, COMP), F32),...  38.3 us

profile of v6, /device:TPU:1, one launch (start us, length us, event | category | flops | bytes accessed | tf_op | source)
XLA Modules:
  0.0 38.9 jit_solution(9356875243011227204)
XLA Ops:
  0.0 38.3 %shard_map.64 = f32[16,64]{1,0:T(8,128)S(1)} custom-call(f32[24,64]{1,0:T(8,128)} %elution_hbm.1, f32[8,64]{1,0:T(8,128)} %loadings_hbm.1, s32[8,64]{1,0:T(8,128)} %shifts_hbm.1, f32[48,128]{1,0:T(8,128)} %bitcast.3, f32[448,128]{1,0:T(8,128)} %constant.2.clone.tables_hbm, bf16[8,192,512]{2,1,0:T(8,128)(2,1)} %intensity_hbm.1), custom_call_target="tpu_custom_call" | custom-call | tf_op jit(solution)/shard_map/pallas_call | solution.py:540
  38.3 0.6 %copy.8 = f32[64,16]{0,1:T(8,128)} copy(f32[64,16]{0,1:T(8,128)S(1)} %bitcast.2) | data formatting | bytes 8192

commit v7 on v6

--- a/solution.py
+++ b/solution.py
@@ -23,9 +23,9 @@
 CHANNELS = 512
 FREQ = 32
 OWN = 16
-SLAB = 1536
+SLAB = 768
 STEPS = (1, 3, 2)
-WINDOW = 512
+WINDOW = 640
 
 
 def transform_tables():
@@ -109,6 +109,9 @@
     toeplitz,
     total,
     window,
+    exchange_send,
+    exchange_recv,
+    models,
     gram_send,
     gram_core,
     gram_x,
@@ -123,8 +126,7 @@
     second_send,
     third_send,
     own_recv,
-    swap_send,
-    swap_recv,
+    exchange_sem,
     gram_sems,
     num_sem,
 ):
@@ -158,28 +160,24 @@
         load.start()
     barrier = pltpu.get_barrier_semaphore()
 
-    for step in range(8):
-        pl.semaphore_signal(
-            barrier,
-            inc=1,
-            device_id=at(x, y, (1 - z_hi) * 4 + step % 4, step // 4),
-            device_id_type=MESH,
+    def greet(device):
+        pl.semaphore_signal(barrier, inc=1, device_id=device, device_id_type=MESH)
+
+    for step in (4, 3, 5, 2, 6, 1, 7):
+        for core_at in range(2):
+            greet(at(x, y, (z_mine + step) % 8, core_at))
+    for step in (2, 1, 3):
+        greet((freq, ((y + step) % 4) * 2 + z_hi))
+        greet((((x + step) % 4) * 8 + freq % 8, mz))
+    greet(partner)
+    loads[0].wait()
+    for group in range(3):
+        start = 4 * group
+        packed_rows[group] = jnp.concatenate(
+            [elution_ref[start : start + 4, :], elution_ref[12 + start : 16 + start, :]], axis=1
         )
-    for step in range(1, 4):
-        pl.semaphore_signal(
-            barrier, inc=1, device_id=(freq, ((y + step) % 4) * 2 + z_hi), device_id_type=MESH
-        )
-    def greet(step, carry):
-        pl.semaphore_signal(barrier, inc=1, device_id=((freq + step) % FREQ, mz), device_id_type=MESH)
-        return carry
-
-    lax.fori_loop(1, FREQ, greet, 0)
-    loads[0].wait()
-    own_rows = elution_ref[...]
-    beside = jnp.concatenate([own_rows[16:24], own_rows[16:24]], axis=0)
-    packed_rows[...] = jnp.concatenate([own_rows[0:16], beside], axis=1)
-
-    pl.semaphore_wait(barrier, FREQ - 1 + 3 + 8)
+
+    pl.semaphore_wait(barrier, 14 + 6 + 1)
 
     def remote(source, target, send, recv, device):
         return pltpu.make_async_remote_copy(
@@ -189,51 +187,50 @@
     z_copies = [
         remote(
             packed_rows,
-            gathered.at[z_lo, core],
+            gathered.at[z_hi, z_lo % 2, core],
             z_send.at[step],
-            z_recv.at[z_lo, core],
-            at(x, y, (z_mine + step) % 8, z_hi),
+            z_recv.at[z_hi, z_lo % 2, core],
+            at(x, y, (z_mine + step) % 8, z_lo // 2),
         )
         for step in range(8)
     ]
-    for copy in z_copies[1:]:
-        copy.start()
-
-    @pl.when(z_hi != core)
+    for step in (4, 3, 5, 2, 6, 1, 7):
+        z_copies[step].start()
+
+    @pl.when(z_lo // 2 != core)
     def _():
         z_copies[0].start()
 
-    @pl.when(z_hi == core)
+    @pl.when(z_lo // 2 == core)
     def _():
-        gathered[z_lo, core] = packed_rows[...]
-
-    close = z_lo // 2
-    near = close * (1 - abs(z_hi - core)) + (1 - close) * abs(z_hi - core)
-
-    def half_of(colour_is_own, half):
-        return near if (half == 0) == colour_is_own else 1 - near
-
-    left16 = lax.broadcasted_iota(jnp.int32, (16, LANES), 1) < 64
-    left8 = left16[:8]
-
-    def merge(half):
-        for index in range(2):
-            source = 2 * half_of(True, half) + index
-            for source_core in range(2):
-                itself = jnp.logical_and(z_hi == core, jnp.logical_and(z_lo == source, core == source_core))
-
-                @pl.when(jnp.logical_not(itself))
-                def _(source=source, source_core=source_core):
-                    spot = gathered.at[source, source_core]
-                    remote(packed_rows, spot, z_send.at[0], z_recv.at[source, source_core], partner).wait_recv()
-
-            zero, one = gathered[source, 0], gathered[source, 1]
-            blocks[core, x, y, source, 0:16] = jnp.where(left16, zero, half_turn(one))
-            blocks[core, x, y, source, 16:24] = jnp.where(left8, half_turn(zero[:8]), one[:8])
-
-    def piece(colour_is_own, colour, dx, dy, half):
-        start = 2 * half_of(colour_is_own, half)
-        return blocks.at[colour, (x + dx) % 4, (y + dy) % 4, pl.ds(start, 2)]
+        gathered[z_hi, z_lo % 2, core] = packed_rows[...]
+
+    left4 = lax.broadcasted_iota(jnp.int32, (4, LANES), 1) < 64
+
+    def merge():
+        for zh_at in range(2):
+            for zl_at in range(2):
+                for source_core in range(2):
+                    spot = gathered.at[zh_at, zl_at, source_core]
+                    itself = jnp.logical_and(
+                        jnp.logical_and(z_lo // 2 == core, z_hi == zh_at),
+                        jnp.logical_and(z_lo % 2 == zl_at, core == source_core),
+                    )
+
+                    @pl.when(jnp.logical_not(itself))
+                    def _(spot=spot, sem=z_recv.at[zh_at, zl_at, source_core]):
+                        remote(packed_rows, spot, z_send.at[0], sem, partner).wait_recv()
+
+        for zh_at in range(2):
+            for zl_at in range(2):
+                for group in range(3):
+                    zero, one = gathered[zh_at, zl_at, 0, group], gathered[zh_at, zl_at, 1, group]
+                    start = 24 * zh_at + 4 * group
+                    blocks[x, y, zl_at, start : start + 4] = jnp.where(left4, zero, half_turn(one))
+                    blocks[x, y, zl_at, start + 12 : start + 16] = jnp.where(left4, half_turn(zero), one)
+
+    def piece(dx, dy):
+        return blocks.at[(x + dx) % 4, (y + dy) % 4]
 
     class Colour:
         def __init__(self, colour):
@@ -242,63 +239,55 @@
         def offsets(self, a, b):
             return (a, b) if self.colour == 0 else (b, a)
 
-        def send(self, a, b, a_step, b_step, half, sem):
-            source = piece(True, self.colour, *self.offsets(a, b), half)
+        def send(self, a, b, a_step, b_step, sem):
+            source = piece(*self.offsets(a, b))
             to_x, to_y = self.offsets(a_step, b_step)
             dx, dy = self.offsets((a - a_step) % 4, (b - b_step) % 4)
             device = at((x + to_x) % 4, (y + to_y) % 4, z_mine, self.colour)
-            remote(source, source, sem, own_recv.at[dx, dy, half], device).start()
-
-        def second(self, half):
+            remote(source, source, sem, own_recv.at[dx, dy], device).start()
+
+        def second(self):
             for step in STEPS:
-                self.send(0, 0, step, 0, half, second_send)
-
-        def third(self, a, half):
-            for step in STEPS:
-                self.send(a, 0, 0, step, half, third_send)
-
-        def arrived(self, a, b, half):
-            dx, dy = self.offsets(a, b)
-            spot = piece(True, self.colour, dx, dy, half)
-            remote(spot, spot, swap_send, own_recv.at[dx, dy, half], partner).wait_recv()
-            if b == 0:
-                self.third(a, half)
-            self.swap(dx, dy, half)
-
-        def swap(self, dx, dy, half):
-            spot = piece(True, self.colour, dx, dy, half)
-            remote(spot, spot, swap_send, swap_recv.at[dx, dy, half], partner).start()
-
-        def open_up(self, half):
+                self.send(0, 0, step, 0, second_send)
+
+        def third(self, a, steps):
+            for step in steps:
+                self.send(a, 0, 0, step, third_send)
+
+        def open_up(self):
             if self.colour == 0:
-                self.third(0, half)
-                self.second(half)
+                self.third(0, STEPS)
+                self.second()
             else:
-                self.second(half)
-                self.third(0, half)
-            self.swap(0, 0, half)
-
-        def first_arrivals(self, half):
-            for a, b in ((3, 0), (1, 0), (0, 3), (0, 1), (2, 0), (0, 2)):
-                self.arrived(a, b, half)
+                self.second()
+                self.third(0, STEPS[:2])
+
+        def pass_on(self):
+            for a in (3, 1, 2):
+                arrived(*self.offsets(a, 0))
+                self.third(a, STEPS if self.colour == 0 else STEPS[:2])
+            if self.colour == 1:
+                for a in (0, 3, 1, 2):
+                    self.third(a, STEPS[2:])
+
+    def arrived(dx, dy):
+        spot = piece(dx, dy)
+        remote(spot, spot, second_send, own_recv.at[dx, dy], partner).wait_recv()
 
     def for_each_core(action):
         for colour in range(2):
             pl.when(core == colour)(functools.partial(action, Colour(colour)))
 
-    def swapped(dx):
-        for half in range(2):
-            for dy in range(4):
-                spot = piece(False, 1 - core, dx, dy, half)
-                remote(spot, spot, swap_send, swap_recv.at[dx, dy, half], partner).wait_recv()
-
-    def arrivals(spots):
-        def action(colour):
-            for half in range(2):
-                for dx, dy in spots:
-                    colour.arrived(*colour.offsets(dx, dy), half)
-
-        return action
+    def slab_arrived(dx):
+        @pl.when(core == 0)
+        def _():
+            for dy in (3, 1, 2):
+                arrived(dx, dy)
+
+        @pl.when(jnp.logical_and(core == 1, dx != 0))
+        def _():
+            for dy in (0, 3, 1, 2):
+                arrived(dx, dy)
 
     loads[1].wait()
     loads[2].wait()
@@ -327,103 +316,125 @@
 
     lax.fori_loop(0, 16, build, turned(2, 15))
 
-    merge(0)
-    for_each_core(lambda colour: colour.open_up(0))
-    merge(1)
-    for_each_core(lambda colour: colour.open_up(1))
+    merge()
+    for_each_core(lambda colour: colour.open_up())
     slab[0:128, :] = jnp.zeros((128, LANES), BF16)
     slab[128 + SLAB : 256 + SLAB, :] = jnp.zeros((128, LANES), BF16)
-    for_each_core(lambda colour: colour.first_arrivals(0))
-    for_each_core(lambda colour: colour.first_arrivals(1))
-
-    left = lax.broadcasted_iota(jnp.int32, (24, LANES), 1) < 64
-    begin = ((freq * 3 + 96 - 4) // 2) % ROWS
-
-    def unpack(dx):
-        x_at = (x + dx) % 4
-
+    total[...] = jnp.zeros_like(total)
+    for_each_core(lambda colour: colour.pass_on())
+
+    left48 = lax.broadcasted_iota(jnp.int32, (48, LANES), 1) < 64
+    begin = ((freq // 2) * 3 + ROWS - 2) % ROWS
+
+    def unpack(x_at):
         def unpack_one(zl_at, carry):
             low_rows, high_rows = [], []
             for y_at in range(4):
-                for colour in range(2):
-                    block = blocks[colour, x_at, y_at, zl_at]
-                    rounded = block.astype(BF16).astype(F32)
-                    rest = block - rounded
-                    low_rows.append(jnp.where(left, rounded, half_turn(rest)))
-                    high_rows.append(jnp.where(left, half_turn(rounded), rest))
+                block = blocks[x_at, y_at, zl_at]
+                rounded = block.astype(BF16).astype(F32)
+                rest = block - rounded
+                low_rows.append(jnp.where(left48, rounded, half_turn(rest)))
+                high_rows.append(jnp.where(left48, half_turn(rounded), rest))
             rows = jnp.concatenate(low_rows + high_rows, axis=0).astype(BF16)
             start = pl.multiple_of(zl_at * 384, 128)
             slab[pl.ds(128 + start, 384), :] = rows
             profile[pl.ds(pl.multiple_of(x_at * SLAB, 128) + start, 384), :] = rows
             return carry
 
-        lax.fori_loop(0, 4, unpack_one, 0)
-
-    def filtered(dx):
-        first = ((x + dx) % 4) * 12 - 1 + 2 * ROWS - begin
+        lax.fori_loop(0, 2, unpack_one, 0)
+
+    def filtered(x_at):
+        first = x_at * 12 + core * 6 - 1 + 2 * ROWS - begin
         lines = []
         for part in range(2):
-            for row_block in (0, 2):
+            for row_block in (0, 2, 4):
                 lines.append(
                     jnp.concatenate(
-                        [toeplitz[part, (first + step - row_block) % ROWS] for step in range(13)], axis=1
+                        [toeplitz[part, (first + step - row_block) % ROWS] for step in range(7)], axis=1
                     )
                 )
         rows = jnp.concatenate([slab[0 : 128 + SLAB, :], slab[128 : 256 + SLAB, :]], axis=1)
-        value = jnp.dot(jnp.concatenate(lines, axis=0), rows, preferred_element_type=F32)
-        total[...] += value
-
-    total[...] = jnp.zeros_like(total)
+        total[...] += jnp.dot(jnp.concatenate(lines, axis=0), rows, preferred_element_type=F32)
+
+    left224 = lax.broadcasted_iota(jnp.int32, (224, LANES), 1) < 64
+
+    def exchange(kind):
+        return remote(exchange_send.at[kind], exchange_recv.at[kind], exchange_sem.at[kind, 0], exchange_sem.at[kind, 1], partner)
+
+    def give(kind):
+        start = pl.multiple_of((1 - core) * 192, 64)
+        top = window[kind, pl.ds(start, 224), :]
+        exchange_send[kind] = jnp.where(left224, top, window[kind, pl.ds(start + 224, 224), :])
+        exchange(kind).start()
+
+    def take(kind):
+        exchange(kind).wait()
+        both = exchange_recv[kind]
+        turned_both = half_turn(both)
+        top = jnp.where(left224, both, turned_both)
+        rest = jnp.where(left224, turned_both, both)
+        own = window[kind, pl.ds(pl.multiple_of(core * 192, 64), 448), :]
+        return own + jnp.concatenate([top, rest], axis=0)
+
+    def give_profile():
+        for row_block in range(5):
+            at_block = (begin + row_block) % ROWS
+            cut = pl.ds(row_block * 128, 128)
+            held_here = (at_block % 12) // 6 == core
+
+            @pl.when(held_here)
+            def _(at_block=at_block, cut=cut):
+                start = pl.multiple_of((at_block // 12) * SLAB + (at_block % 6) * 128, 128)
+                value = profile[pl.ds(start, 128), :].astype(F32)
+                window[1, cut, :] = value + half_turn(value)
+
+            @pl.when(jnp.logical_not(held_here))
+            def _(cut=cut):
+                window[1, cut, :] = jnp.zeros((128, LANES), F32)
+
+        give(1)
 
     def slab_step(index, carry):
         dx = jnp.where(index == 0, 0, jnp.where(index == 1, 3, index - 1))
-        swapped(dx)
-        unpack(dx)
-        filtered(dx)
-
-        @pl.when(index == 0)
-        def _():
-            for_each_core(arrivals(((3, 3), (3, 1), (3, 2), (1, 3), (1, 1), (1, 2))))
+        x_at = (x + dx) % 4
+        slab_arrived(dx)
+        unpack(x_at)
+        filtered(x_at)
 
         @pl.when(index == 1)
         def _():
-            for_each_core(arrivals(((2, 3), (2, 1), (2, 2))))
+            give_profile()
 
         return carry
 
     lax.fori_loop(0, 4, slab_step, 0)
 
-    for row_block in range(4):
+    for row_block in range(5):
         base = (row_block // 2) * 128
         cut = pl.ds((row_block % 2) * 128, 128)
-        value = total[pl.ds(base, 128), cut] + total[pl.ds(256 + base, 128), cut]
+        value = total[pl.ds(base, 128), cut] + total[pl.ds(384 + base, 128), cut]
         window[0, pl.ds(row_block * 128, 128), :] = value + half_turn(value)
-        start = pl.multiple_of(((begin + row_block) % ROWS) * 128, 128)
-        value = profile[pl.ds(start, 128), :].astype(F32)
-        window[1, pl.ds(row_block * 128, 128), :] = value + half_turn(value)
-
-    skip = pl.multiple_of((freq % 2) * 64, 64)
+    give(0)
     for load in loads[3:]:
         load.wait()
-    filtered_rows = window[0, pl.ds(skip, 448), :]
-    plain_rows = window[1, pl.ds(skip, 448), :]
+
+    def by_pair(ref, pair_at):
+        return jnp.concatenate([ref[2 * pair_at : 2 * pair_at + 1], ref[2 * pair_at + 1 : 2 * pair_at + 2]], axis=1)
+
+    plain_rows = take(1)
+    for pair_at in range(RUNS // 2):
+        moved = shifted(plain_rows, 255 - by_pair(shifts_ref, pair_at)) * by_pair(loadings_ref, pair_at)
+        high, low = split(moved)
+        models[pair_at] = jnp.concatenate([high, low], axis=1)
+    filtered_rows = take(0)
     quad = jnp.zeros((256, 256), F32)
     numer = jnp.zeros((COMP, CHANNELS), F32)
     stacks = []
     for pair_at in range(RUNS // 2):
-        amount = jnp.concatenate([shifts_ref[2 * pair_at : 2 * pair_at + 1], shifts_ref[2 * pair_at + 1 : 2 * pair_at + 2]], axis=1)
-        gain = jnp.concatenate(
-            [loadings_ref[2 * pair_at : 2 * pair_at + 1], loadings_ref[2 * pair_at + 1 : 2 * pair_at + 2]], axis=1
-        )
-        moved = jnp.transpose(shifted(filtered_rows, 255 - amount) * gain)
-        model_high, model_low = split(shifted(plain_rows, 255 - amount) * gain)
-        high, low = split(moved)
+        moved = shifted(filtered_rows, 255 - by_pair(shifts_ref, pair_at)) * by_pair(loadings_ref, pair_at)
+        high, low = split(jnp.transpose(moved))
         stacks.append((high, low))
-        quad = quad + jnp.dot(
-            jnp.concatenate([high, low], axis=0),
-            jnp.concatenate([model_high, model_low], axis=1),
-            preferred_element_type=F32,
-        )
+        quad = quad + jnp.dot(jnp.concatenate([high, low], axis=0), models[pair_at], preferred_element_type=F32)
     corner = quad[:128, :128] + quad[:128, 128:] + quad[128:, :128]
     gram_own = corner[:64] + half_turn(corner[64:])
     left32 = lax.broadcasted_iota(jnp.int32, (32, LANES), 1) < 64
@@ -466,12 +477,12 @@
     for copy in z_copies[1:]:
         copy.wait_send()
 
-    @pl.when(z_hi != core)
+    @pl.when(z_lo // 2 != core)
     def _():
         z_copies[0].wait_send()
 
-    for spot, sem in ((blocks.at[0, 0, 0:3], second_send), (blocks.at[0, 0:3], third_send), (blocks.at[0], swap_send)):
-        remote(spot, spot, sem, z_recv.at[0, 0], partner).wait_send()
+    for spot, sem in ((blocks.at[0, 0:3], second_send), (blocks.at[0:3], third_send)):
+        remote(spot, spot, sem, exchange_sem.at[0, 1], partner).wait_send()
 
     for copy in x_copies:
         copy.wait()
@@ -549,16 +560,19 @@
             pltpu.VMEM((ROWS, LANES), F32),
             pltpu.VMEM((448, LANES), F32),
             pltpu.VMEM((RUNS, BLOCK, CHANNELS), BF16),
-            pltpu.VMEM((16, LANES), F32),
-            pltpu.VMEM((4, 2, 16, LANES), F32),
-            pltpu.VMEM((2, 4, 4, 4, 24, LANES), F32),
-            pltpu.VMEM((LENGTH, LANES), BF16),
+            pltpu.VMEM((3, 4, LANES), F32),
+            pltpu.VMEM((2, 2, 2, 3, 4, LANES), F32),
+            pltpu.VMEM((4, 4, 2, 48, LANES), F32),
+            pltpu.VMEM((4 * SLAB, LANES), BF16),
             pltpu.VMEM((SLAB + 256, LANES), BF16),
             pltpu.VMEM((3, 16, LANES), F32),
             pltpu.VMEM((LANES, LANES), F32),
             pltpu.VMEM((2, ROWS, LANES, LANES), BF16),
-            pltpu.VMEM((512, 256), F32),
+            pltpu.VMEM((768, 256), F32),
             pltpu.VMEM((2, WINDOW, LANES), F32),
+            pltpu.VMEM((2, 224, LANES), F32),
+            pltpu.VMEM((2, 224, LANES), F32),
+            pltpu.VMEM((RUNS // 2, BLOCK, 2 * LANES), BF16),
             pltpu.VMEM((3, 32, LANES), F32),
             pltpu.VMEM((32, LANES), F32),
             pltpu.VMEM((3, 32, LANES), F32),
@@ -569,12 +583,11 @@
             pltpu.VMEM((FREQ // 2, 8, LANES), F32),
             dma((6,)),
             dma((8,)),
-            dma((4, 2)),
+            dma((2, 2, 2)),
             dma,
             dma,
-            dma((4, 4, 2)),
-            dma,
-            dma((4, 4, 2)),
+            dma((4, 4)),
+            dma((2, 2)),
             dma((14,)),
             dma((4,)),
         ],

time: 39 us -> 37.8 us (0.969)
  Pallas kernels: 38.3 us -> 37.1 us
    pallas_call x1, Pallas kernels: 38.3 us -> 37.1 us  [on_device(): pl.pallas_call(kernel, out_shape=jax.ShapeDtypeStruct((OWN, COMP), F32),...]
where the time goes in v7:
time: 37.8 us; the launch traced here: 37.7 us
  Pallas kernels  37.1 us (98%)
  local copies, waits for them, and re-layouts  0.6 us (2%)
    pallas_call x1, Pallas kernels, on_device(): pl.pallas_call(kernel, out_shape=jax.ShapeDtypeStruct((OWN, COMP), F32),...  37.1 us

profile of v7, /device:TPU:1, one launch (start us, length us, event | category | flops | bytes accessed | tf_op | source)
XLA Modules:
  0.0 37.7 jit_solution(6755260933954215938)
XLA Ops:
  0.0 37.1 %shard_map.64 = f32[16,64]{1,0:T(8,128)S(1)} custom-call(f32[24,64]{1,0:T(8,128)} %elution_hbm.1, f32[8,64]{1,0:T(8,128)} %loadings_hbm.1, s32[8,64]{1,0:T(8,128)} %shifts_hbm.1, f32[48,128]{1,0:T(8,128)} %bitcast.3, f32[448,128]{1,0:T(8,128)} %constant.2.clone.tables_hbm, bf16[8,192,512]{2,1,0:T(8,128)(2,1)} %intensity_hbm.1), custom_call_target="tpu_custom_call" | custom-call | tf_op jit(solution)/shard_map/pallas_call | solution.py:551
  37.1 0.6 %copy.8 = f32[64,16]{0,1:T(8,128)} copy(f32[64,16]{0,1:T(8,128)S(1)} %bitcast.2) | data formatting | bytes 8192

commit v8 on v7

--- a/solution.py
+++ b/solution.py
@@ -255,12 +255,8 @@
                 self.send(a, 0, 0, step, third_send)
 
         def open_up(self):
-            if self.colour == 0:
-                self.third(0, STEPS)
-                self.second()
-            else:
-                self.second()
-                self.third(0, STEPS[:2])
+            self.second()
+            self.third(0, STEPS if self.colour == 0 else STEPS[:2])
 
         def pass_on(self):
             for a in (3, 1, 2):
@@ -484,6 +480,9 @@
     for spot, sem in ((blocks.at[0, 0:3], second_send), (blocks.at[0:3], third_send)):
         remote(spot, spot, sem, exchange_sem.at[0, 1], partner).wait_send()
 
+    num_swap.wait()
+    num_half[...] = num_send[core] + num_core[...]
+    lax.fori_loop(1, FREQ // 2, send_num, 0)
     for copy in x_copies:
         copy.wait()
     gram_send[2] = (gram_send[1] + gram_x[0]) + (gram_x[1] + gram_x[2])
@@ -498,46 +497,61 @@
         )
         copy.start()
         z_grams.append(copy)
-    num_swap.wait()
-    num_half[...] = num_send[core] + num_core[...]
-    lax.fori_loop(1, FREQ // 2, send_num, 0)
     for copy in z_grams:
         copy.wait()
     packed = (gram_send[2] + gram_z[0]) + (gram_z[1] + gram_z[2])
 
     row64 = lax.broadcasted_iota(jnp.int32, (COMP, LANES), 0)
     lane64 = lax.broadcasted_iota(jnp.int32, (COMP, LANES), 1)
-    unit = (lane64 == row64 + COMP).astype(F32)
-    matrix = jnp.where(lane64 < COMP, jnp.concatenate([packed, half_turn(packed)], axis=0), unit)
-    def clear(value, top, low, columns, step):
+    row8 = row64[:8]
+    gram = jnp.concatenate([packed, half_turn(packed)], axis=0)
+    diagonal = jnp.where(lane64 == row64, gram, 0.0)
+    scale_rows = jnp.broadcast_to(lax.rsqrt(jnp.sum(diagonal, axis=1, keepdims=True)), gram.shape)
+    scale_lanes = lax.rsqrt(jnp.sum(diagonal, axis=0, keepdims=True))
+    unit = jnp.where(lane64 == row64 + COMP, scale_rows, 0.0)
+    whole = jnp.where(lane64 < COMP, gram * scale_rows * scale_lanes, unit)
+    matrix = [whole[8 * at_ : 8 * at_ + 8] for at_ in range(8)]
+
+    def line(value, step):
+        return value[step // 8][step % 8 : step % 8 + 1]
+
+    def pivot(columns, step):
         one, two = columns
-        one_top, one_low = one[step : step + 1], one[step + 1 : step + 2]
-        two_top, two_low = two[step : step + 1], two[step + 1 : step + 2]
-        scale = 1.0 / (one_top * two_low - two_top * one_low)
-        top_new = (two_low * top - two_top * low) * scale
-        low_new = (one_top * low - one_low * top) * scale
-        rest = value - one * top_new - two * low_new
-        return jnp.where(row64 == step, top_new, jnp.where(row64 == step + 1, low_new, rest))
-
-    for step in range(0, COMP, 4):
-        columns = [jnp.broadcast_to(matrix[:, at_ : at_ + 1], matrix.shape) for at_ in range(step, step + 4)]
-        first_two = columns[:2]
-        last_two = [
-            clear(value, value[step : step + 1], value[step + 1 : step + 2], first_two, step) for value in columns[2:]
+        return line(one, step) * line(two, step + 1) - line(two, step) * line(one, step + 1)
+
+    def clear(value, columns, step, scale):
+        one, two = columns
+        at_, row_at = step // 8, step % 8
+        top, low = line(value, step), line(value, step + 1)
+        top_new = (line(two, step + 1) * top - line(two, step) * low) * scale
+        low_new = (line(one, step) * low - line(one, step + 1) * top) * scale
+        rest = [v - o * top_new - t * low_new for v, o, t in zip(value, one, two)]
+        rest[at_] = jnp.where(row8 == row_at, top_new, jnp.where(row8 == row_at + 1, low_new, rest[at_]))
+        return rest
+
+    for step in range(0, COMP, 8):
+        columns = [
+            [jnp.broadcast_to(block[:, at_ : at_ + 1], block.shape) for block in matrix] for at_ in range(step, step + 8)
         ]
-        matrix = clear(matrix, matrix[step : step + 1], matrix[step + 1 : step + 2], first_two, step)
-        matrix = clear(matrix, matrix[step + 2 : step + 3], matrix[step + 3 : step + 4], last_two, step + 2)
-    inverse = matrix[:, COMP:]
-
+        for at_ in range(step, step + 8, 2):
+            pair, columns = columns[:2], columns[2:]
+            scale = 1.0 / pivot(pair, at_)
+            columns = [clear(value, pair, at_, scale) for value in columns]
+            matrix = clear(matrix, pair, at_, scale)
+    inverse = (jnp.concatenate(matrix, axis=0) * scale_rows)[:, COMP:]
+
+    inverse_both = jnp.concatenate(split(inverse), axis=0)
     others = num_recv.at[0 : FREQ // 2 - 1]
     num_all = remote(others, others, num_sem.at[0], num_sem.at[1], partner)
     num_all.wait_recv()
     num_recv[chip] = num_half[chip]
     summed = jnp.sum(num_recv[...], axis=0)
     own_channels = jnp.concatenate([summed[:, :64], summed[:, 64:]], axis=0)
-    out_ref[...] = lax.dot_general(
-        own_channels, inverse, (((1,), (1,)), ((), ())), precision=HIGHEST, preferred_element_type=F32
+    high, low = split(own_channels)
+    parts = lax.dot_general(
+        jnp.concatenate([high, low], axis=0), inverse_both, (((1,), (1,)), ((), ())), preferred_element_type=F32
     )
+    out_ref[...] = (parts[:OWN, :COMP] + parts[:OWN, COMP:]) + parts[OWN:, :COMP]
 
     num_all.wait_send()
 

time: 37.8 us -> 37.8 us (level)
  no operation moved by 1% of the time
where the time goes in v8:
time: 37.8 us; the launch traced here: 37.7 us
  Pallas kernels  37.1 us (98%)
  local copies, waits for them, and re-layouts  0.6 us (2%)
    pallas_call x1, Pallas kernels, on_device(): pl.pallas_call(kernel, out_shape=jax.ShapeDtypeStruct((OWN, COMP), F32),...  37.1 us

profile of v8, /device:TPU:1, one launch (start us, length us, event | category | flops | bytes accessed | tf_op | source)
XLA Modules:
  0.0 37.7 jit_solution(14754375089622687335)
XLA Ops:
  0.0 37.1 %shard_map.64 = f32[16,64]{1,0:T(8,128)S(1)} custom-call(f32[24,64]{1,0:T(8,128)} %elution_hbm.1, f32[8,64]{1,0:T(8,128)} %loadings_hbm.1, s32[8,64]{1,0:T(8,128)} %shifts_hbm.1, f32[48,128]{1,0:T(8,128)} %bitcast.3, f32[448,128]{1,0:T(8,128)} %constant.2.clone.tables_hbm, bf16[8,192,512]{2,1,0:T(8,128)(2,1)} %intensity_hbm.1), custom_call_target="tpu_custom_call" | custom-call | tf_op jit(solution)/shard_map/pallas_call | solution.py:565
  37.1 0.6 %copy.8 = f32[64,16]{0,1:T(8,128)} copy(f32[64,16]{0,1:T(8,128)S(1)} %bitcast.2) | data formatting | bytes 8192

commit v9 on v8

--- a/solution.py
+++ b/solution.py
@@ -323,7 +323,7 @@
     begin = ((freq // 2) * 3 + ROWS - 2) % ROWS
 
     def unpack(x_at):
-        def unpack_one(zl_at, carry):
+        for zl_at in range(2):
             low_rows, high_rows = [], []
             for y_at in range(4):
                 block = blocks[x_at, y_at, zl_at]
@@ -332,12 +332,9 @@
                 low_rows.append(jnp.where(left48, rounded, half_turn(rest)))
                 high_rows.append(jnp.where(left48, half_turn(rounded), rest))
             rows = jnp.concatenate(low_rows + high_rows, axis=0).astype(BF16)
-            start = pl.multiple_of(zl_at * 384, 128)
-            slab[pl.ds(128 + start, 384), :] = rows
+            start = zl_at * 384
+            slab[128 + start : 512 + start, :] = rows
             profile[pl.ds(pl.multiple_of(x_at * SLAB, 128) + start, 384), :] = rows
-            return carry
-
-        lax.fori_loop(0, 2, unpack_one, 0)
 
     def filtered(x_at):
         first = x_at * 12 + core * 6 - 1 + 2 * ROWS - begin
@@ -428,7 +425,7 @@
     stacks = []
     for pair_at in range(RUNS // 2):
         moved = shifted(filtered_rows, 255 - by_pair(shifts_ref, pair_at)) * by_pair(loadings_ref, pair_at)
-        high, low = split(jnp.transpose(moved))
+        high, low = (jnp.transpose(part) for part in split(moved))
         stacks.append((high, low))
         quad = quad + jnp.dot(jnp.concatenate([high, low], axis=0), models[pair_at], preferred_element_type=F32)
     corner = quad[:128, :128] + quad[:128, 128:] + quad[128:, :128]

time: 37.8 us -> 37.7 us (level)
  no operation moved by 1% of the time
where the time goes in v9:
time: 37.7 us; the launch traced here: 37.5 us
  Pallas kernels  36.9 us (98%)
  local copies, waits for them, and re-layouts  0.6 us (2%)
    pallas_call x1, Pallas kernels, on_device(): pl.pallas_call(kernel, out_shape=jax.ShapeDtypeStruct((OWN, COMP), F32),...  36.9 us

profile of v9, /device:TPU:1, one launch (start us, length us, event | category | flops | bytes accessed | tf_op | source)
XLA Modules:
  0.0 37.5 jit_solution(3950694638993462139)
XLA Ops:
  0.0 36.9 %shard_map.64 = f32[16,64]{1,0:T(8,128)S(1)} custom-call(f32[24,64]{1,0:T(8,128)} %elution_hbm.1, f32[8,64]{1,0:T(8,128)} %loadings_hbm.1, s32[8,64]{1,0:T(8,128)} %shifts_hbm.1, f32[48,128]{1,0:T(8,128)} %bitcast.3, f32[448,128]{1,0:T(8,128)} %constant.2.clone.tables_hbm, bf16[8,192,512]{2,1,0:T(8,128)(2,1)} %intensity_hbm.1), custom_call_target="tpu_custom_call" | custom-call | tf_op jit(solution)/shard_map/pallas_call | solution.py:562
  36.9 0.6 %copy.8 = f32[64,16]{0,1:T(8,128)} copy(f32[64,16]{0,1:T(8,128)S(1)} %bitcast.2) | data formatting | bytes 8192

commit v10 on v9

--- a/solution.py
+++ b/solution.py
@@ -394,7 +394,7 @@
         unpack(x_at)
         filtered(x_at)
 
-        @pl.when(index == 1)
+        @pl.when(index == jnp.where(z_lo == 0, 1, 0))
         def _():
             give_profile()
 

time: 37.7 us -> 37.7 us (level)
  no operation moved by 1% of the time
where the time goes in v10:
time: 37.7 us; the launch traced here: 37.5 us
  Pallas kernels  36.9 us (98%)
  local copies, waits for them, and re-layouts  0.6 us (2%)
    pallas_call x1, Pallas kernels, on_device(): pl.pallas_call(kernel, out_shape=jax.ShapeDtypeStruct((OWN, COMP), F32),...  36.9 us

profile of v10, /device:TPU:1, one launch (start us, length us, event | category | flops | bytes accessed | tf_op | source)
XLA Modules:
  0.0 37.5 jit_solution(13336048852193950503)
XLA Ops:
  0.0 36.9 %shard_map.64 = f32[16,64]{1,0:T(8,128)S(1)} custom-call(f32[24,64]{1,0:T(8,128)} %elution_hbm.1, f32[8,64]{1,0:T(8,128)} %loadings_hbm.1, s32[8,64]{1,0:T(8,128)} %shifts_hbm.1, f32[48,128]{1,0:T(8,128)} %bitcast.3, f32[448,128]{1,0:T(8,128)} %constant.2.clone.tables_hbm, bf16[8,192,512]{2,1,0:T(8,128)(2,1)} %intensity_hbm.1), custom_call_target="tpu_custom_call" | custom-call | tf_op jit(solution)/shard_map/pallas_call | solution.py:562
  36.9 0.6 %copy.8 = f32[64,16]{0,1:T(8,128)} copy(f32[64,16]{0,1:T(8,128)S(1)} %bitcast.2) | data formatting | bytes 8192
